TPU v7x, 32 devices: a whole 2x2x4 slice. The times are simulated.
32 devices in a mesh: shard: 2 (over y), ctx: 4 (over z), tp: 4 (over x, core).
Axes of the slice: x: 2, y: 2, z: 4, core: 2. Of those that a mesh axis runs over, the one named last changes fastest.
Arguments:
- inputs: bfloat16 [4, 1024, 768], P('shard', ('ctx', 'tp')), may hold values from -6 to 6
- seg_ids: int32 [4, 1024], P('shard', 'ctx'), may hold values from 0 to 7, never falling along the last dimension, each value on 1 to 512 neighbouring positions
- feature_map: float32 [12, 64, 256], P('tp'), may hold values from -6 to 6
- w_query: bfloat16 [768, 768], P(('shard', 'ctx'), 'tp'), may hold values from -0.21875 to 0.21875
- w_key: bfloat16 [768, 768], P(('shard', 'ctx'), 'tp'), may hold values from -0.21875 to 0.21875
- w_value: bfloat16 [768, 768], P(('shard', 'ctx'), 'tp'), may hold values from -0.21875 to 0.21875
- w_out: bfloat16 [768, 768], P('tp', ('shard', 'ctx')), may hold values from -0.875 to 0.875
- gain_attn: float32 [768], replicated, may hold values from 0.5 to 1.5
- shift_attn: float32 [768], replicated, may hold values from -3 to 3
- w_up: bfloat16 [768, 3072], P(('shard', 'ctx'), 'tp'), may hold values from -0.21875 to 0.21875
- bias_up: float32 [3072], P('tp'), may hold values from -3 to 3
- w_down: bfloat16 [3072, 768], P('tp', ('shard', 'ctx')), may hold values from -0.109375 to 0.109375
- bias_down: float32 [768], replicated, may hold values from -3 to 3
- gain_ffn: float32 [768], replicated, may hold values from 0.5 to 1.5
- shift_ffn: float32 [768], replicated, may hold values from -3 to 3
- cotangent: bfloat16 [4, 1024, 768], P('shard', ('ctx', 'tp')), may hold values from -6 to 6
Outputs:
- outputs: bfloat16 [4, 1024, 768], P('shard', ('ctx', 'tp'))
- grad_inputs: bfloat16 [4, 1024, 768], P('shard', ('ctx', 'tp'))
- grad_query: float32 [768, 768], P(('shard', 'ctx'), 'tp')
- grad_key: float32 [768, 768], P(('shard', 'ctx'), 'tp')
- grad_value: float32 [768, 768], P(('shard', 'ctx'), 'tp')
- grad_out: float32 [768, 768], P('tp', ('shard', 'ctx'))
- grad_gain_attn: float32 [768], replicated
- grad_shift_attn: float32 [768], replicated
- grad_up: float32 [768, 3072], P(('shard', 'ctx'), 'tp')
- grad_bias_up: float32 [3072], P('tp')
- grad_down: float32 [3072, 768], P('tp', ('shard', 'ctx'))
- grad_bias_down: float32 [768], replicated
- grad_gain_ffn: float32 [768], replicated
- grad_shift_ffn: float32 [768], replicated
Inputs may be any that keep to these rules, and one draw needn't show every extreme that they name: `seg_ids`: within each sequence the numbers never fall, every number below 8 occurs, and no document has more than 512 tokens.
All inputs are finite; a program needn't handle non-finite values.
Results may differ from a plain program's by a relative error of at most 0.025.
Values may be sent and summed in bfloat16 or wider, within the bound.
A program may use at most 128 MiB of HBM per device.

v0:
```python
import jax
import jax.numpy as jnp
from jax import lax
from jax.sharding import PartitionSpec as P

HEAD_DIM = 64
FEATS = 256
FF = 3072
SEGS = 8


highest = lax.Precision.HIGHEST
root_half = 0.7071067811865476
inv_root_tau = 0.3989422804014327
norm_eps = 1e-05


def gelu_value(upper):
    return upper * 0.5 * (1.0 + lax.erf(upper * root_half))


def gelu_slope(upper):
    return 0.5 * (1.0 + lax.erf(upper * root_half)) + upper * inv_root_tau * jnp.exp(
        -0.5 * upper * upper
    )


def layer_norm(hidden_in, gain_vec, shift_vec):
    mean_val = jnp.mean(hidden_in, -1, keepdims=True)
    centred = hidden_in - mean_val
    inv_std = lax.rsqrt(jnp.mean(centred * centred, -1, keepdims=True) + norm_eps)
    normed = centred * inv_std
    return (normed * gain_vec + shift_vec, normed, inv_std)


def norm_back(grad_in, normed, inv_std, gain_vec):
    scaled = grad_in * gain_vec
    grad_hidden = inv_std * (
        scaled
        - jnp.mean(scaled, -1, keepdims=True)
        - normed * jnp.mean(scaled * normed, -1, keepdims=True)
    )
    return (grad_hidden, jnp.sum(grad_in * normed, (0, 1)), jnp.sum(grad_in, (0, 1)))


def features(projected, omega_local):
    seq_count, ctx_rows, width = projected.shape
    heads_here = omega_local.shape[0]
    scaled = projected.reshape(seq_count, ctx_rows, heads_here, HEAD_DIM) * HEAD_DIM ** (-0.25)
    angles = jnp.einsum("schd,hdm->schm", scaled, omega_local, precision=highest)
    squares = 0.5 * jnp.sum(scaled * scaled, -1, keepdims=True)
    return (jnp.exp(angles - squares) * FEATS ** (-0.5), scaled)


def feature_back(grad_phi, phi_full, scaled, omega_local):
    grad_angle = grad_phi * phi_full
    grad_scaled = jnp.einsum("schm,hdm->schd", grad_angle, omega_local, precision=highest)
    grad_scaled = grad_scaled - scaled * jnp.sum(grad_angle, -1, keepdims=True)
    seq_count, ctx_rows, heads_here, head_width = scaled.shape
    return (grad_scaled * HEAD_DIM ** (-0.25)).reshape(seq_count, ctx_rows, heads_here * head_width)


def spread_rows(mask_low, left):
    ctx_rows, heads_here, feat_count = left.shape
    wide = mask_low[:, None, :, None] * left[:, :, None, :]
    return wide.reshape(ctx_rows, heads_here, -1)


def segment_outer(operands):
    mask_low, left, right = operands
    return jnp.einsum(
        "chx,che->hxe", spread_rows(mask_low, left), right, preferred_element_type=jnp.float32
    )


def segment_apply(operands):
    mask_low, left, table = operands
    return jnp.einsum(
        "chx,hxe->che", spread_rows(mask_low, left), table, preferred_element_type=jnp.float32
    )


def segment_back(operands):
    mask_full, left, table = operands
    ctx_rows, heads_here, width = left.shape
    seg_count = mask_full.shape[1]
    wide = jnp.einsum("che,hxe->chx", left, table, preferred_element_type=jnp.float32)
    wide = wide.reshape(ctx_rows, heads_here, seg_count, -1)
    return jnp.sum(wide * mask_full[:, None, :, None], 2)


def inner_product(left, right):
    return lax.dot_general(
        left, right, (((0,), (0,)), ((), ())), preferred_element_type=jnp.float32
    )


def right_transposed(left, right):
    return lax.dot_general(
        left, right, (((1,), (1,)), ((), ())), preferred_element_type=jnp.float32
    )


def per_device(
    inputs,
    seg_ids,
    feature_map,
    w_query,
    w_key,
    w_value,
    w_out,
    gain_attn,
    shift_attn,
    w_up,
    bias_up,
    w_down,
    bias_down,
    gain_ffn,
    shift_ffn,
    cotangent,
):
    full_query, full_key, full_value, full_up, full_out, full_down = (
        lax.all_gather(w_query, ("shard", "ctx"), axis=0, tiled=True),
        lax.all_gather(w_key, ("shard", "ctx"), axis=0, tiled=True),
        lax.all_gather(w_value, ("shard", "ctx"), axis=0, tiled=True),
        lax.all_gather(w_up, ("shard", "ctx"), axis=0, tiled=True),
        lax.all_gather(w_out, ("shard", "ctx"), axis=1, tiled=True),
        lax.all_gather(w_down, ("shard", "ctx"), axis=1, tiled=True),
    )
    seq_count, row_share, width = inputs.shape
    rows_all = lax.all_gather(inputs, "tp", axis=1, tiled=True)
    ctx_rows = rows_all.shape[1]
    token_count = seq_count * ctx_rows
    flat = rows_all.reshape(token_count, width)
    heads_here = feature_map.shape[0]
    head_cols = heads_here * HEAD_DIM
    query_proj = jnp.dot(flat, full_query, preferred_element_type=jnp.float32).reshape(
        seq_count, ctx_rows, head_cols
    )
    key_proj = jnp.dot(flat, full_key, preferred_element_type=jnp.float32).reshape(
        seq_count, ctx_rows, head_cols
    )
    value_low = jnp.dot(flat, full_value, preferred_element_type=jnp.float32).astype(jnp.bfloat16)
    value_low = value_low.reshape(seq_count, ctx_rows, head_cols)
    value_four = value_low.reshape(seq_count, ctx_rows, heads_here, HEAD_DIM)
    phi_query, scaled_query = features(query_proj, feature_map)
    phi_key, scaled_key = features(key_proj, feature_map)
    phq_low = phi_query.astype(jnp.bfloat16)
    phk_low = phi_key.astype(jnp.bfloat16)
    matches = seg_ids[:, :, None] == jnp.arange(SEGS, dtype=jnp.int32)[None, None, :]
    mask_low = matches.astype(jnp.bfloat16)
    mask_full = matches.astype(jnp.float32)
    kv_part = lax.map(segment_outer, (mask_low, phk_low, value_four))
    z_part = jnp.einsum("scg,schm->shgm", mask_low, phk_low, preferred_element_type=jnp.float32)
    kv_sum, z_sum = lax.psum((kv_part, z_part), "ctx")
    kv_low = kv_sum.astype(jnp.bfloat16)
    numer = lax.map(segment_apply, (mask_low, phq_low, kv_low))
    phq_wide = phq_low.astype(jnp.float32)
    denom = jnp.sum(
        jnp.einsum("schm,shgm->schg", phq_wide, z_sum, precision=highest)
        * mask_full[:, :, None, :],
        -1,
    )
    mixed = numer / denom[..., None]
    mixed_low = mixed.astype(jnp.bfloat16).reshape(seq_count, ctx_rows, head_cols)
    piece = mixed_low
    attn_sum = jnp.swapaxes(
        lax.psum_scatter(
            jnp.einsum("scf,fd->csd", piece, full_out, preferred_element_type=jnp.float32),
            "tp",
            scatter_dimension=0,
            tiled=True,
        ),
        0,
        1,
    )
    first, normed_one, inv_one = layer_norm(
        inputs.astype(jnp.float32) + attn_sum, gain_attn, shift_attn
    )
    first_low = first.astype(jnp.bfloat16)
    first_rows = lax.all_gather(first_low, "tp", axis=1, tiled=True)
    first_flat = first_rows.reshape(token_count, width)
    upper = jnp.dot(first_flat, full_up, preferred_element_type=jnp.float32) + bias_up
    ffn_here = upper.shape[1]
    hidden_low = gelu_value(upper).astype(jnp.bfloat16)
    hidden_three = hidden_low.reshape(seq_count, ctx_rows, ffn_here)
    piece = hidden_three
    branch = jnp.swapaxes(
        lax.psum_scatter(
            jnp.einsum("scf,fd->csd", piece, full_down, preferred_element_type=jnp.float32),
            "tp",
            scatter_dimension=0,
            tiled=True,
        ),
        0,
        1,
    )
    final, normed_two, inv_two = layer_norm(first + branch + bias_down, gain_ffn, shift_ffn)
    outputs = final.astype(jnp.bfloat16)
    full_query, full_key, full_value, full_up, full_out, full_down = (
        lax.all_gather(w_query, ("shard", "ctx"), axis=0, tiled=True),
        lax.all_gather(w_key, ("shard", "ctx"), axis=0, tiled=True),
        lax.all_gather(w_value, ("shard", "ctx"), axis=0, tiled=True),
        lax.all_gather(w_up, ("shard", "ctx"), axis=0, tiled=True),
        lax.all_gather(w_out, ("shard", "ctx"), axis=1, tiled=True),
        lax.all_gather(w_down, ("shard", "ctx"), axis=1, tiled=True),
    )
    grad_final = cotangent.astype(jnp.float32)
    grad_two, grad_gain_ffn, grad_shift_ffn = norm_back(grad_final, normed_two, inv_two, gain_ffn)
    grad_bias_down = jnp.sum(grad_two, (0, 1))
    grad_two_rows = lax.all_gather(grad_two.astype(jnp.bfloat16), "tp", axis=1, tiled=True)
    grad_two_flat = grad_two_rows.reshape(token_count, width)
    grad_hidden = right_transposed(grad_two_flat, full_down)
    grad_upper = (grad_hidden * gelu_slope(upper)).astype(jnp.bfloat16)
    grad_down = inner_product(hidden_low, grad_two_flat)
    grad_up = inner_product(first_flat, grad_upper)
    grad_bias_local = jnp.sum(grad_upper.astype(jnp.float32), 0)
    grad_upper_three = grad_upper.reshape(seq_count, ctx_rows, ffn_here)
    piece = grad_upper_three
    grad_first = grad_two + jnp.swapaxes(
        lax.psum_scatter(
            jnp.einsum("scf,df->csd", piece, full_up, preferred_element_type=jnp.float32),
            "tp",
            scatter_dimension=0,
            tiled=True,
        ),
        0,
        1,
    )
    grad_one, grad_gain_attn, grad_shift_attn = norm_back(
        grad_first, normed_one, inv_one, gain_attn
    )
    grad_one_rows = lax.all_gather(grad_one.astype(jnp.bfloat16), "tp", axis=1, tiled=True)
    grad_one_flat = grad_one_rows.reshape(token_count, width)
    grad_out = inner_product(mixed_low.reshape(token_count, head_cols), grad_one_flat)
    grad_mixed = right_transposed(grad_one_flat, full_out).reshape(
        seq_count, ctx_rows, heads_here, HEAD_DIM
    )
    grad_numer = (grad_mixed / denom[..., None]).astype(jnp.bfloat16)
    grad_denom = -jnp.sum(grad_mixed * mixed, -1) / denom
    kv_grad_part = lax.map(segment_outer, (mask_low, phq_low, grad_numer))
    z_grad_part = jnp.einsum(
        "scg,schm->shgm", mask_full, phq_wide * grad_denom[..., None], precision=highest
    )
    kv_grad, z_grad = (
        lax.psum(kv_grad_part.astype(jnp.bfloat16), "ctx").astype(jnp.float32),
        lax.psum(z_grad_part.astype(jnp.bfloat16), "ctx").astype(jnp.float32),
    )
    kv_grad_low = kv_grad.astype(jnp.bfloat16)
    grad_phq = lax.map(segment_back, (mask_full, grad_numer, kv_low))
    grad_phq = grad_phq + grad_denom[..., None] * jnp.einsum(
        "scg,shgm->schm", mask_full, z_sum, precision=highest
    )
    grad_phk = lax.map(segment_back, (mask_full, value_four, kv_grad_low))
    grad_phk = grad_phk + jnp.einsum("scg,shgm->schm", mask_full, z_grad, precision=highest)
    grad_value_rows = lax.map(segment_apply, (mask_low, phk_low, kv_grad_low)).astype(jnp.bfloat16)
    grad_value_rows = grad_value_rows.reshape(seq_count, ctx_rows, head_cols)
    grad_query_rows = feature_back(grad_phq, phi_query, scaled_query, feature_map).astype(
        jnp.bfloat16
    )
    grad_key_rows = feature_back(grad_phk, phi_key, scaled_key, feature_map).astype(jnp.bfloat16)
    grad_query = inner_product(flat, grad_query_rows.reshape(token_count, head_cols))
    grad_key = inner_product(flat, grad_key_rows.reshape(token_count, head_cols))
    grad_value = inner_product(flat, grad_value_rows.reshape(token_count, head_cols))
    total = jnp.einsum(
        "scf,df->csd", grad_query_rows, full_query, preferred_element_type=jnp.float32
    )
    total = total + jnp.einsum(
        "scf,df->csd", grad_key_rows, full_key, preferred_element_type=jnp.float32
    )
    grad_rows = jnp.swapaxes(
        lax.psum_scatter(
            (
                total
                + jnp.einsum(
                    "scf,df->csd", grad_value_rows, full_value, preferred_element_type=jnp.float32
                )
            ).astype(jnp.bfloat16),
            "tp",
            scatter_dimension=0,
            tiled=True,
        ).astype(jnp.float32),
        0,
        1,
    )
    grad_inputs = (grad_one + grad_rows).astype(jnp.bfloat16)
    grad_query, grad_key, grad_value, grad_up, grad_out, grad_down = (
        lax.psum_scatter(grad_query, ("shard", "ctx"), scatter_dimension=0, tiled=True),
        lax.psum_scatter(grad_key, ("shard", "ctx"), scatter_dimension=0, tiled=True),
        lax.psum_scatter(grad_value, ("shard", "ctx"), scatter_dimension=0, tiled=True),
        lax.psum_scatter(grad_up, ("shard", "ctx"), scatter_dimension=0, tiled=True),
        lax.psum_scatter(grad_out, ("shard", "ctx"), scatter_dimension=1, tiled=True),
        lax.psum_scatter(grad_down, ("shard", "ctx"), scatter_dimension=1, tiled=True),
    )
    tp_index = lax.axis_index("tp")
    padded_bias = lax.dynamic_update_slice(
        jnp.zeros((FF,), jnp.float32), grad_bias_local, (tp_index * ffn_here,)
    )
    grad_gain_attn, grad_shift_attn, grad_gain_ffn, grad_shift_ffn, grad_bias_down, padded_bias = (
        lax.psum(
            (
                grad_gain_attn,
                grad_shift_attn,
                grad_gain_ffn,
                grad_shift_ffn,
                grad_bias_down,
                padded_bias,
            ),
            ("shard", "ctx", "tp"),
        )
    )
    grad_bias_up = lax.dynamic_slice(padded_bias, (tp_index * ffn_here,), (ffn_here,))
    return (
        outputs,
        grad_inputs,
        grad_query,
        grad_key,
        grad_value,
        grad_out,
        grad_gain_attn,
        grad_shift_attn,
        grad_up,
        grad_bias_up,
        grad_down,
        grad_bias_down,
        grad_gain_ffn,
        grad_shift_ffn,
    )


def solution(mesh):
    placed = (
        P("shard", ("ctx", "tp"), None),
        P("shard", "ctx"),
        P("tp", None, None),
        P(("shard", "ctx"), "tp"),
        P(("shard", "ctx"), "tp"),
        P(("shard", "ctx"), "tp"),
        P("tp", ("shard", "ctx")),
        P(),
        P(),
        P(("shard", "ctx"), "tp"),
        P("tp"),
        P("tp", ("shard", "ctx")),
        P(),
        P(),
        P(),
        P("shard", ("ctx", "tp"), None),
    )
    return jax.shard_map(
        per_device,
        mesh=mesh,
        in_specs=placed,
        out_specs=(
            P("shard", ("ctx", "tp"), None),
            P("shard", ("ctx", "tp"), None),
            P(("shard", "ctx"), "tp"),
            P(("shard", "ctx"), "tp"),
            P(("shard", "ctx"), "tp"),
            P("tp", ("shard", "ctx")),
            P(),
            P(),
            P(("shard", "ctx"), "tp"),
            P("tp"),
            P("tp", ("shard", "ctx")),
            P(),
            P(),
            P(),
        ),
        check_vma=False,
    )
```

profile of v0, /device:TPU:0, one launch (start us, length us, event | category | flops | bytes accessed | tf_op | source)
XLA Modules:
  0.0 1010.6 jit_solution(17872332154931087539)
XLA Ops:
  8.1 10.4 %all_gather.36 = bf16[2,256,768]{2,1,0:T(8,128)(2,1)S(1)} all-gather(bf16[2,64,768]{2,1,0:T(8,128)(2,1)} %param.28), channel_id=1, replica_groups=mesh['shard'=2,'ctx'=4,'tp'=4] {'tp'}, dimensions={1}, use_global_device_ids=true | all-gather | bytes 983040 | tf_op jit(solution)/shard_map/all_gather | solution.py:131
  18.5 32.5 %all_gather.37 = bf16[768,192]{1,0:T(8,128)(2,1)S(1)} all-gather(bf16[96,192]{1,0:T(8,128)(2,1)} %param.32), channel_id=1, replica_groups=mesh['shard'=2,'ctx'=4,'tp'=4] {'shard','ctx'}, dimensions={0}, use_global_device_ids=true | all-gather | bytes 331776 | tf_op jit(solution)/shard_map/all_gather | solution.py:124
  56.2 31.7 %all_gather.38 = bf16[768,192]{1,0:T(8,128)(2,1)S(1)} all-gather(bf16[96,192]{1,0:T(8,128)(2,1)S(1)} %copy-done.48), channel_id=1, replica_groups=mesh['shard'=2,'ctx'=4,'tp'=4] {'shard','ctx'}, dimensions={0}, use_global_device_ids=true | all-gather | bytes 331776 | tf_op jit(solution)/shard_map/all_gather | solution.py:125
  92.8 20.8 %while.66 = (s32[]{:T(128)}, f32[2,3,2048,64]{2,3,1,0:T(8,128)}, bf16[2,256,8]{2,1,0:T(8,128)(2,1)S(1)}, bf16[2,256,3,256]{3,1,2,0:T(8,128)(2,1)}, bf16[2,256,3,64]{1,3,2,0:T(8,128)(2,1)}) while((s32[]{:T(128)}, f32[2,3,2048,64]{2,3,1,0:T(8,128)}, bf16[2,256,8]{2,1,0:T(8,128)(2,1)S(1)}, bf16[2,256,3,256]{3,1,2,0:T(8,128)(2,1)}, ...), condition=%wide.region_3.4_spmd.clone, body=%wide.region_2.3_spmd.sunk.clone | while | flops 207618048 | bytes 20427872 | solution.py:153
  96.0 4.2 mul.740
  106.4 4.2 mul.740
  113.6 32.0 %all_gather.39 = bf16[768,192]{1,0:T(8,128)(2,1)S(1)} all-gather(bf16[96,192]{1,0:T(8,128)(2,1)S(1)} %copy-done.49), channel_id=1, replica_groups=mesh['shard'=2,'ctx'=4,'tp'=4] {'shard','ctx'}, dimensions={0}, use_global_device_ids=true | all-gather | bytes 331776 | tf_op jit(solution)/shard_map/all_gather | solution.py:123
  152.1 96.2 %all-reduce.6 = (bf16[2,3,2048,64]{2,3,1,0:T(8,128)(2,1)}, f32[2,3,8,256]{3,2,1,0:T(8,128)S(1)}) all-reduce(f32[2,3,2048,64]{2,3,1,0:T(8,128)} %get-tuple-element.176, f32[2,3,8,256]{3,2,1,0:T(8,128)S(1)} %copy-done.46), channel_id=1, replica_groups=mesh['shard'=2,'ctx'=4,'tp'=4] {'ctx'}, use_global_device_ids=true, to_apply=%region_4.5 | all-reduce | flops 798720 | bytes 4816896 | tf_op jit(solution)/shard_map/psum | solution.py:155
  248.4 19.4 %while.67 = (s32[]{:T(128)}, f32[2,256,3,64]{1,3,2,0:T(8,128)}, bf16[2,3,2048,64]{2,3,1,0:T(8,128)(2,1)}, bf16[2,256,8]{2,1,0:T(8,128)(2,1)S(1)}, bf16[2,256,3,256]{3,1,2,0:T(8,128)(2,1)}) while((s32[]{:T(128)}, f32[2,256,3,64]{1,3,2,0:T(8,128)}, bf16[2,3,2048,64]{2,3,1,0:T(8,128)(2,1)}, bf16[2,256,8]{2,1,0:T(8,128)(2,1)S(1)}, ...), condition=%wide.region_6.7_spmd.clone, body=%wide.region_5.6_spmd.sunk.clone | while | flops 202899456 | bytes 31536224 | solution.py:157
  268.7 31.9 %all_gather.40 = bf16[192,768]{0,1:T(8,128)(2,1)S(1)} all-gather(bf16[192,96]{0,1:T(8,128)(2,1)S(1)} %copy.105), channel_id=1, replica_groups=mesh['shard'=2,'ctx'=4,'tp'=4] {'shard','ctx'}, dimensions={1}, use_global_device_ids=true | all-gather | bytes 331776 | tf_op jit(solution)/shard_map/all_gather | solution.py:127
  305.4 26.8 %reduce-scatter.19.cloned.1.call-done = f32[64,2,768]{2,0,1:T(8,128)} async-done(((f32[256,2,768]{2,0,1:T(8,128)}), f32[64,2,768]{2,0,1:T(8,128)}) %reduce-scatter.19.cloned.1.call-update) | async-done | bytes 393232 | tf_op jit(solution)/shard_map/reduce_scatter | solution.py:168
  334.3 8.0 all_gather.41
  342.3 5.7 all-gather.3.cloned.1.call-done
  351.3 38.5 %all-gather.5.cloned.1.call-done = bf16[768,768]{0,1:T(8,128)(2,1)} async-done(((bf16[768,96]{0,1:T(8,128)(2,1)}), bf16[768,768]{0,1:T(8,128)(2,1)}) %all-gather.5.cloned.1.call-update) | async-done | bytes 1179664 | tf_op jit(solution)/shard_map/all_gather | solution.py:128
  393.2 26.5 %reduce-scatter.21.cloned.1.call-done = f32[64,2,768]{2,0,1:T(8,128)} async-done(((f32[256,2,768]{2,0,1:T(8,128)}), f32[64,2,768]{2,0,1:T(8,128)}) %reduce-scatter.21.cloned.1.call-update) | async-done | bytes 393232 | tf_op jit(solution)/shard_map/reduce_scatter | solution.py:189
  421.7 8.1 all_gather.44
  437.6 25.5 %reduce-scatter.23.cloned.1.call-done = f32[64,2,768]{2,0,1:T(8,128)} async-done(((f32[256,2,768]{2,0,1:T(8,128)}), f32[64,2,768]{2,0,1:T(8,128)}) %reduce-scatter.23.cloned.1.call-update) | async-done | bytes 393232 | tf_op jit(solution)/shard_map/reduce_scatter | solution.py:221
  466.1 8.0 all_gather.45
  475.9 20.0 %while.69 = (s32[]{:T(128)}, bf16[2,3,2048,64]{2,3,1,0:T(8,128)(2,1)}, bf16[2,256,8]{2,1,0:T(8,128)(2,1)S(1)}, bf16[2,256,3,256]{3,1,2,0:T(8,128)(2,1)}, bf16[2,256,3,64]{1,3,2,0:T(8,128)(2,1)}) while((s32[]{:T(128)}, bf16[2,3,2048,64]{2,3,1,0:T(8,128)(2,1)}, bf16[2,256,8]{2,1,0:T(8,128)(2,1)S(1)}, ...), condition=%wide.region_26.27_spmd.clone, body=%wide.region_25.26_spmd.sunk.clone | while | flops 207618048 | bytes 20427872 | solution.py:241
  478.9 4.2 mul.752
  488.9 4.2 mul.752
  497.5 7.0 while.68
  508.1 20.3 %psum.73 = bf16[2,3,8,256]{3,2,1,0:T(8,128)(2,1)S(1)} all-reduce(bf16[2,3,8,256]{3,2,1,0:T(8,128)(2,1)S(1)} %fusion.107), channel_id=1, replica_groups=mesh['shard'=2,'ctx'=4,'tp'=4] {'ctx'}, use_global_device_ids=true, to_apply=%region_31.32 | all-reduce | flops 12288 | bytes 49152 | tf_op jit(solution)/shard_map/psum | solution.py:247
  532.6 33.8 %all-reduce.5.cloned.1.call-done = bf16[2,3,2048,64]{2,3,1,0:T(8,128)(2,1)} async-done(((bf16[2,3,2048,64]{2,3,1,0:T(8,128)(2,1)}), bf16[2,3,2048,64]{2,3,1,0:T(8,128)(2,1)}) %all-reduce.5.cloned.1.call-update) | async-done | bytes 1572880 | tf_op jit(solution)/shard_map/psum | solution.py:246
  567.7 7.5 while.70
  580.1 19.7 %while.71 = (s32[]{:T(128)}, bf16[2,256,3,64]{1,3,2,0:T(8,128)(2,1)}, bf16[2,3,2048,64]{2,3,1,0:T(8,128)(2,1)}, bf16[2,256,8]{2,1,0:T(8,128)(2,1)S(1)}, bf16[2,256,3,256]{3,1,2,0:T(8,128)(2,1)}) while((s32[]{:T(128)}, bf16[2,256,3,64]{1,3,2,0:T(8,128)(2,1)}, bf16[2,3,2048,64]{2,3,1,0:T(8,128)(2,1)}, ...), condition=%wide.region_34.35_spmd.clone, body=%wide.region_33.34_spmd.sunk.clone | while | flops 202899456 | bytes 33109144 | solution.py:256
  615.9 40.8 %all-reduce = (f32[768]{0:T(1024)}, f32[768]{0:T(1024)}, f32[3072]{0:T(1024)S(1)}, f32[768]{0:T(1024)}, f32[768]{0:T(1024)}, /*index=5*/f32[768]{0:T(1024)}) all-reduce(f32[768]{0:T(1024)S(1)} %copy-done.69, f32[768]{0:T(1024)S(1)} %copy-done.68, ...), channel_id=1, replica_groups=mesh['shard'=2,'ctx'=4,'tp'=4] {'shard','ctx','tp'}, use_global_device_ids=true, to_apply=%region_41.42 | all-reduce | flops 6912 | bytes 55296 | tf_op jit(solution)/shard_map/psum | solution.py:300
  660.9 63.8 %reduce-scatter.31.cloned.1.call-done = f32[96,192]{1,0:T(8,128)} async-done(((f32[768,192]{1,0:T(8,128)}), f32[96,192]{1,0:T(8,128)}) %reduce-scatter.31.cloned.1.call-update) | async-done | bytes 73744
  724.7 72.9 %reduce-scatter.29.cloned.1.call-done = f32[768,96]{0,1:T(8,128)} async-done(((f32[768,768]{0,1:T(8,128)}), f32[768,96]{0,1:T(8,128)}) %reduce-scatter.29.cloned.1.call-update) | async-done | bytes 294928 | tf_op jit(solution)/shard_map/reduce_scatter | solution.py:293
  797.6 73.1 %reduce-scatter.27.cloned.1.call-done = f32[96,768]{1,0:T(8,128)} async-done(((f32[768,768]{1,0:T(8,128)}), f32[96,768]{1,0:T(8,128)}) %reduce-scatter.27.cloned.1.call-update) | async-done | bytes 294928 | tf_op jit(solution)/shard_map/reduce_scatter | solution.py:291
  870.7 66.1 %reduce-scatter.33.cloned.1.call-done = f32[96,192]{1,0:T(8,128)} async-done(((f32[768,192]{1,0:T(8,128)}), f32[96,192]{1,0:T(8,128)}) %reduce-scatter.33.cloned.1.call-update) | async-done | bytes 73744
  936.8 66.2 %reduce-scatter.35.cloned.1.call-done = f32[96,192]{1,0:T(8,128)} async-done(((f32[768,192]{1,0:T(8,128)}), f32[96,192]{1,0:T(8,128)}) %reduce-scatter.35.cloned.1.call-update) | async-done | bytes 73744
  (358 shorter events, 157.7 us)
Async XLA Ops:
  8.0 44.3 %copy-start = (f32[3,64,256]{2,1,0:T(8,128)S(1)}, f32[3,64,256]{2,1,0:T(8,128)}, u32[]{:S(2)}) copy-start(f32[3,64,256]{2,1,0:T(8,128)} %param.30) | copy-start | bytes 589828
  8.0 324.2 %reduce-scatter.19.cloned.1.call-start = ((), (), s32[]{:S(2)}) async-start(), calls=%async_computation.10 | async-start | bytes 1966080 | tf_op jit(solution)/shard_map/reduce_scatter | solution.py:168
  18.5 69.4 %copy-start.4 = (bf16[2,256,768]{2,1,0:T(8,128)(2,1)}, bf16[2,256,768]{2,1,0:T(8,128)(2,1)S(1)}, u32[]{:S(2)}) copy-start(bf16[2,256,768]{2,1,0:T(8,128)(2,1)S(1)} %all_gather.36) | copy-start | bytes 2359300
  56.2 33.6 %copy-start.56 = (s32[2,256]{1,0:T(2,128)S(1)}, s32[2,256]{1,0:T(2,128)}, u32[]{:S(2)}) copy-start(s32[2,256]{1,0:T(2,128)} %param.29) | copy-start | bytes 6148
  150.8 97.5 %copy-start.24 = (bf16[2,256,3,256]{1,3,0,2:T(8,128)(2,1)}, bf16[2,256,3,256]{1,3,0,2:T(8,128)(2,1)S(1)}, u32[]{:S(2)}) copy-start(bf16[2,256,3,256]{1,3,0,2:T(8,128)(2,1)S(1)} %get-tuple-element.414) | copy-start | bytes 2359300
  267.8 34.8 %copy-start.45 = (f32[2,256,3,64]{1,3,2,0:T(8,128)S(1)}, f32[2,256,3,64]{1,3,2,0:T(8,128)}, u32[]{:S(2)}) copy-start(f32[2,256,3,64]{1,3,2,0:T(8,128)} %get-tuple-element.177) | copy-start | bytes 1179652
  302.6 29.7 %copy-start.42 = (bf16[2,64,768]{2,1,0:T(8,128)(2,1)S(1)}, bf16[2,64,768]{2,1,0:T(8,128)(2,1)}, u32[]{:S(2)}) copy-start(bf16[2,64,768]{2,1,0:T(8,128)(2,1)} %param.28) | copy-start | bytes 589828
  304.2 30.0 %copy-start.47 = (f32[768]{0:T(1024)S(1)}, f32[768]{0:T(1024)}, u32[]{:S(2)}) copy-start(f32[768]{0:T(1024)} %param.35) | copy-start | bytes 9220
  304.2 30.0 %copy-start.61 = (f32[768]{0:T(1024)S(1)}, f32[768]{0:T(1024)}, u32[]{:S(2)}) copy-start(f32[768]{0:T(1024)} %param.36) | copy-start | bytes 9220
  304.2 43.8 %all-gather.3.cloned.1.call-start = ((), (), s32[]{:S(2)}) async-start(), calls=%async_computation.11 | async-start | bytes 1327104 | tf_op jit(solution)/shard_map/all_gather | solution.py:126
  304.8 85.1 %all-gather.5.cloned.1.call-start = ((), (), s32[]{:S(2)}) async-start(), calls=%async_computation.12 | async-start | bytes 1327104 | tf_op jit(solution)/shard_map/all_gather | solution.py:128
  305.4 114.3 %reduce-scatter.21.cloned.1.call-start = ((), (), s32[]{:S(2)}) async-start(), calls=%async_computation.13 | async-start | bytes 1966080 | tf_op jit(solution)/shard_map/reduce_scatter | solution.py:189
  333.4 132.6 %copy-start.6 = (f32[2,64,768]{2,1,0:T(8,128)}, f32[2,64,768]{2,1,0:T(8,128)S(1)}, u32[]{:S(2)}) copy-start(f32[2,64,768]{2,1,0:T(8,128)S(1)} %get-tuple-element.395) | copy-start | bytes 1179652
  351.3 41.8 %copy-start.28 = (bf16[512,768]{1,0:T(8,128)(2,1)}, bf16[512,768]{1,0:T(8,128)(2,1)S(1)}, u32[]{:S(2)}) copy-start(bf16[512,768]{1,0:T(8,128)(2,1)S(1)} %get-tuple-element.416) | copy-start | bytes 2359300
  393.2 70.0 %reduce-scatter.23.cloned.1.call-start = ((), (), s32[]{:S(2)}) async-start(), calls=%async_computation.14 | async-start | bytes 1966080 | tf_op jit(solution)/shard_map/reduce_scatter | solution.py:221
  434.4 28.7 %copy-start.51 = (f32[768]{0:T(1024)S(1)}, f32[768]{0:T(1024)}, u32[]{:S(2)}) copy-start(f32[768]{0:T(1024)} %param.41) | copy-start | bytes 9220
  434.4 28.7 %copy-start.54 = (f32[2,64]{1,0:T(2,128)S(1)}, f32[2,64]{1,0:T(2,128)}, u32[]{:S(2)}) copy-start(f32[2,64]{1,0:T(2,128)} %copy-done.52) | copy-start | bytes 1540
  434.5 131.9 %all-reduce.5.cloned.1.call-start = ((), (), s32[]{:S(2)}) async-start(), calls=%async_computation.15 | async-start | bytes 3145728 | tf_op jit(solution)/shard_map/psum | solution.py:246
  495.9 161.5 %reduce-scatter.37.cloned.1.call-start = ((), (), s32[]{:S(2)}) async-start(), calls=%async_computation.22 | async-start | bytes 884736
  530.9 36.8 %copy-start.33 = (bf16[2,256,3,64]{1,3,2,0:T(8,128)(2,1)}, bf16[2,256,3,64]{1,3,2,0:T(8,128)(2,1)S(1)}, u32[]{:S(2)}) copy-start(bf16[2,256,3,64]{1,3,2,0:T(8,128)(2,1)S(1)} %fusion.96) | copy-start | bytes 589828
  532.5 35.3 %copy-start.9 = (bf16[2,256,3,64]{1,3,2,0:T(8,128)(2,1)S(1)}, bf16[2,256,3,64]{1,3,2,0:T(8,128)(2,1)}, u32[]{:S(2)}) copy-start(bf16[2,256,3,64]{1,3,2,0:T(8,128)(2,1)} %get-tuple-element.797) | copy-start | bytes 589828
  532.5 126.5 %reduce-scatter.25.cloned.1.call-start = ((), (), s32[]{:S(2)}) async-start(), calls=%async_computation.16 | async-start | bytes 983040 | tf_op jit(solution)/shard_map/reduce_scatter | solution.py:272
  603.3 121.3 %reduce-scatter.31.cloned.1.call-start = ((), (), s32[]{:S(2)}) async-start(), calls=%async_computation.19 | async-start | bytes 884736
  605.2 192.4 %reduce-scatter.29.cloned.1.call-start = ((), (), s32[]{:S(2)}) async-start(), calls=%async_computation.18 | async-start | bytes 2654208 | tf_op jit(solution)/shard_map/reduce_scatter | solution.py:293
  607.5 263.2 %reduce-scatter.27.cloned.1.call-start = ((), (), s32[]{:S(2)}) async-start(), calls=%async_computation.17 | async-start | bytes 2654208 | tf_op jit(solution)/shard_map/reduce_scatter | solution.py:291
  611.1 325.7 %reduce-scatter.33.cloned.1.call-start = ((), (), s32[]{:S(2)}) async-start(), calls=%async_computation.20 | async-start | bytes 884736
  613.5 389.5 %reduce-scatter.35.cloned.1.call-start = ((), (), s32[]{:S(2)}) async-start(), calls=%async_computation.21 | async-start | bytes 884736
  614.2 44.8 %copy-start.7 = (f32[2,64,768]{2,1,0:T(8,128)S(1)}, f32[2,64,768]{2,1,0:T(8,128)}, u32[]{:S(2)}) copy-start(f32[2,64,768]{2,1,0:T(8,128)} %copy-done.6) | copy-start | bytes 1179652
  614.2 44.8 %copy-start.21 = (f32[2,64,768]{2,1,0:T(8,128)S(1)}, f32[2,64,768]{2,1,0:T(8,128)}, u32[]{:S(2)}) copy-start(f32[2,64,768]{2,1,0:T(8,128)} %copy-done.20) | copy-start | bytes 1179652
  614.3 44.8 %copy-start.55 = (f32[2,64]{1,0:T(2,128)S(1)}, f32[2,64]{1,0:T(2,128)}, u32[]{:S(2)}) copy-start(f32[2,64]{1,0:T(2,128)} %copy-done.52) | copy-start | bytes 1540
  614.3 44.8 %copy-start.75 = (f32[2,64]{1,0:T(2,128)S(1)}, f32[2,64]{1,0:T(2,128)}, u32[]{:S(2)}) copy-start(f32[2,64]{1,0:T(2,128)} %copy-done.74) | copy-start | bytes 1540
  614.3 44.8 %copy-start.77 = (f32[2,64]{1,0:T(2,128)S(1)}, f32[2,64]{1,0:T(2,128)}, u32[]{:S(2)}) copy-start(f32[2,64]{1,0:T(2,128)} %copy-done.76) | copy-start | bytes 1540
  (71 other events, 565.6 us)
Sparse Core Ops, SparseCore 0:
  304.3 27.8 reduce-scatter.18
  393.3 26.3 reduce-scatter.20
  434.5 28.5 reduce-scatter.22
Sparse Core Ops, SparseCore 1:
  306.8 41.2 all-gather.2
  350.0 39.8 all-gather.4
  496.0 70.3 all-reduce.4
  569.7 62.6 reduce-scatter.36
  634.9 22.6 reduce-scatter.24
  661.5 63.1 reduce-scatter.30
  728.6 68.9 reduce-scatter.28
  801.5 69.1 reduce-scatter.26
  874.4 62.3 reduce-scatter.32
  940.7 62.3 reduce-scatter.34
where the time goes:
time: 1020 us; the launch traced here: 1010 us
  waiting for transfers between devices  500 us (49%)
  blocking collectives  320 us (31%)
  local copies, waits for them, and re-layouts  85.6 us (8%)
  matrix products  73.6 us (7%)
  between operations  16.6 us (2%)
  other arithmetic  13 us (1%)
    unnamed x17, waiting for transfers between devices  197 us
    psum x1, blocking collectives, per_device(): kv_sum, z_sum = lax.psum((kv_part, z_part), 'ctx')  96.2 us
    reduce_scatter x1, waiting for transfers between devices, per_device(): lax.psum_scatter(grad_up, ('shard', 'ctx'), scatter_dimension=0, tiled=True)  73.1 us
    reduce_scatter x1, waiting for transfers between devices, per_device(): lax.psum_scatter(grad_down, ('shard', 'ctx'), scatter_dimension=1, tiled=...  72.9 us
    mul x40, local copies, waits for them, and re-layouts, spread_rows(): wide = mask_low[:, None, :, None] * left[:, :, None, :]  51.8 us
    psum x1, blocking collectives, per_device(): lax.psum((grad_gain_attn, grad_shift_attn, grad_gain_ffn, grad_shift_ffn,...  40.8 us
    all_gather x1, waiting for transfers between devices, per_device(): lax.all_gather(w_down, ('shard', 'ctx'), axis=1, tiled=True)  38.5 us
    psum x1, waiting for transfers between devices, per_device(): lax.psum(kv_grad_part.astype(jnp.bfloat16), 'ctx').astype(jnp.float32)  33.8 us
  transfers between devices with their start and end apart: 13, of which 11 were waited for; matrix products, arithmetic and copies ran while one was open for 7% of the time, Pallas kernels for 0%

commit v1 on v0

--- a/solution.py
+++ b/solution.py
@@ -1,6 +1,8 @@
 import jax
 import jax.numpy as jnp
 from jax import lax
+from jax.experimental import pallas as pl
+from jax.experimental.pallas import tpu as pltpu
 from jax.sharding import PartitionSpec as P
 
 HEAD_DIM = 64
@@ -328,6 +330,912 @@
     )
 
 
+BF = jnp.bfloat16
+F32 = jnp.float32
+MESH_ID = pl.DeviceIdType.MESH
+TAB = 80
+SUBS = 3
+
+
+def nn(left, right):
+    return lax.dot_general(left, right, (((1,), (0,)), ((), ())), preferred_element_type=F32)
+
+
+def nt(left, right):
+    return lax.dot_general(left, right, (((1,), (1,)), ((), ())), preferred_element_type=F32)
+
+
+def tn(left, right):
+    return lax.dot_general(left, right, (((0,), (0,)), ((), ())), preferred_element_type=F32)
+
+
+def lanes_of(shape):
+    return lax.broadcasted_iota(jnp.int32, shape, 1)
+
+
+def norm_stats(hidden_in):
+    centred = hidden_in - jnp.mean(hidden_in, -1, keepdims=True)
+    inv_std = lax.rsqrt(jnp.mean(centred * centred, -1, keepdims=True) + norm_eps)
+    return centred * inv_std, inv_std
+
+
+def norm_grad(grad_in, normed, inv_std, gain_vec):
+    scaled = grad_in * gain_vec
+    return inv_std * (
+        scaled
+        - jnp.mean(scaled, -1, keepdims=True)
+        - normed * jnp.mean(scaled * normed, -1, keepdims=True)
+    )
+
+
+def layer_kernel(
+    x_ref, seg_ref, om_ref, wq_ref, wk_ref, wv_ref, wo_ref, ga_ref, sa_ref, wu_ref, bu_ref, wd_ref,
+    bd_ref, gf_ref, sf_ref, cot_ref,
+    out_ref, gin_ref, ok_ref, ov_ref, oq_ref, oo_ref, ou_ref, od_ref, small_ref,
+    X, FI, G2, G1, WK, WV, WQ, WO, WU, WD, OWN_O, OWN_D, P, HID, SLOPE, GUP,
+    FIRST, NORM1, INV1, GH2, GH1,
+    RQ, RK, VX, PQF, PKF, PQ, PK, SS, MSK, CM, SEGZ,
+    OM1, OM2, OMT,
+    MIX, DEN, GX, GKL, GVL, GM, GM3, GV3, RGK, RGV, RGQ, MIXC,
+    TBS, TBR, COMB, GCOMB,
+    SIBS, SIBR, XS, XR,
+    GON, GOW, YSN, YSW, YRN, YRW, ZSN, ZSW, ZRN, ZRW,
+    ARS, ARR, ARZ,
+    ag_s, ag_r, ra_s, ra_r, seg_s, seg_r, wz_s, wz_r, wy_s, wy_r, wc_s, wc_r, wf_s, wf_r, gy_s, gy_r, gz_s, gz_r, gc_s, gc_r, tb_s, tb_r, ar_s, ar_r,
+):
+    y = lax.axis_index("shard")
+    z = lax.axis_index("ctx")
+    t = lax.axis_index("tp")
+    sib_t, far_t = t + 1 - 2 * (t % 2), 3 - t
+    sib = {"tp": sib_t}
+    far = {"tp": far_t}
+    yp = {"shard": 1 - y}
+
+    def along(d):
+        return {"ctx": (z + d) % 4}
+
+    def block_rows(yy, zz):
+        return pl.ds(pl.multiple_of((yy * 4 + zz) * 96, 96), 96)
+
+    def copy(src, dst, send, recv, where):
+        return pltpu.make_async_remote_copy(
+            src_ref=src, dst_ref=dst, send_sem=send, recv_sem=recv, device_id=where,
+            device_id_type=MESH_ID,
+        )
+
+    barrier = pltpu.get_barrier_semaphore()
+    for where in (sib, far, yp, along(1), along(2), along(3)):
+        pl.semaphore_signal(barrier, inc=1, device_id=where, device_id_type=MESH_ID)
+    pl.semaphore_wait(barrier, 6)
+
+    def chunk(tt):
+        return pl.ds(pl.multiple_of(tt * 64, 64), 64)
+
+    def ag_desc(op, buf, s, which):
+        rows = chunk(far_t) if which == 2 else chunk(t)
+        where = far if which == 1 else sib
+        return copy(
+            buf.at[s, rows, :], buf.at[s, rows, :], ag_s.at[op, s, which], ag_r.at[op, s, which], where
+        )
+
+    def ag_start(op, buf, s):
+        ag_desc(op, buf, s, 1).start()
+        ag_desc(op, buf, s, 0).start()
+
+    def ag_pass(op, buf, s):
+        ag_desc(op, buf, s, 1).wait_recv()
+        ag_desc(op, buf, s, 2).start()
+
+    def ag_wait(op, buf, s):
+        ag_desc(op, buf, s, 0).wait_recv()
+        ag_desc(op, buf, s, 2).wait_recv()
+
+    def sib_desc(op, s, part):
+        return copy(
+            SIBS.at[op, s, part], SIBR.at[op, s, part], ra_s.at[op, s, part], ra_r.at[op, s, part], sib
+        )
+
+    def xrs_desc(op, s):
+        return copy(XS.at[op, s], XR.at[op, s], ra_s.at[op, s, 2], ra_r.at[op, s, 2], far)
+
+    def part_rows(s, tt):
+        return P[s, chunk(tt), :]
+
+    def rs_start(op, s):
+        SIBS[op, s, 0] = part_rows(s, (t + 2) % 4).astype(BF)
+        sib_desc(op, s, 0).start()
+        SIBS[op, s, 1] = part_rows(s, sib_t).astype(BF)
+        sib_desc(op, s, 1).start()
+
+    def rs_mid(op, s):
+        sib_desc(op, s, 0).wait_recv()
+        XS[op, s] = (part_rows(s, far_t) + SIBR[op, s, 0].astype(F32)).astype(BF)
+        xrs_desc(op, s).start()
+
+    def rs_fin(op, s):
+        sib_desc(op, s, 1).wait_recv()
+        kept = part_rows(s, t) + SIBR[op, s, 1].astype(F32)
+        xrs_desc(op, s).wait_recv()
+        return kept + XR[op, s].astype(F32)
+
+    gathered = (WK, WV, WQ, WO, WU, WD)
+    mine = (wk_ref, wv_ref, wq_ref, OWN_O, wu_ref, OWN_D)
+
+    def wz_desc(i, d):
+        dst = gathered[i].at[block_rows(y, z), :]
+        return copy(mine[i], dst, wz_s.at[i, d - 1], wz_r.at[i, d - 1], along(d))
+
+    def wy_desc(i, d):
+        dst = gathered[i].at[block_rows(y, (z + 4 - d) % 4), :]
+        return copy(mine[i] if d == 0 else dst, dst, wy_s.at[i, d], wy_r.at[i, d], yp)
+
+    def step_of(way):
+        return 1 - 2 * way
+
+    def came(way, j):
+        return z > j if way == 0 else z + j < 3
+
+    def goes(way, j):
+        return (z >= j) & (z < 3) if way == 0 else (z + j <= 3) & (z > 0)
+
+    def wc_desc(i, way, j):
+        dst = gathered[i].at[block_rows(y, (z + 4 - j * step_of(way)) % 4), :]
+        src = mine[i] if j == 0 else dst
+        return copy(src, dst, wc_s.at[i - 4, way, j], wc_r.at[i - 4, way, j], along(4 + step_of(way)))
+
+    def wf_desc(i, way, j):
+        part = gathered[i].at[block_rows(y, (z + 4 - (j + 1) * step_of(way)) % 4), :]
+        return copy(part, part, wf_s.at[i - 4, way, j], wf_r.at[i - 4, way, j], yp)
+
+    def w_send(i):
+        if i < 4:
+            for d in (2, 1, 3):
+                wz_desc(i, d).start()
+        else:
+            for way in range(2):
+
+                @pl.when(goes(way, 0))
+                def _():
+                    wc_desc(i, way, 0).start()
+
+        wy_desc(i, 0).start()
+
+    def w_pass(i):
+        for d in (2, 1, 3):
+            wz_desc(i, d).wait_recv()
+            wy_desc(i, d).start()
+
+    def w_relay(i, j):
+        for way in range(2):
+
+            @pl.when(came(way, j))
+            def _():
+                wc_desc(i, way, j).wait_recv()
+
+            if j < 2:
+
+                @pl.when(goes(way, j + 1))
+                def _():
+                    wc_desc(i, way, j + 1).start()
+
+            @pl.when(came(way, j))
+            def _():
+                wf_desc(i, way, j).start()
+
+    def w_wait(i):
+        wy_desc(i, 0).wait_recv()
+        if i < 4:
+            for d in (1, 2, 3):
+                wy_desc(i, d).wait_recv()
+            return
+        for way in range(2):
+            for j in range(3):
+
+                @pl.when(came(way, j))
+                def _():
+                    wf_desc(i, way, j).wait_recv()
+
+    w_send(0)
+    w_send(1)
+    own = block_rows(y, z)
+    for s in range(2):
+        X[s, chunk(t), :] = x_ref[s]
+        ag_start(0, X, s)
+    w_send(2)
+    TBR[...] = jnp.zeros_like(TBR)
+    COMB[...] = jnp.zeros_like(COMB)
+    GCOMB[...] = jnp.zeros_like(GCOMB)
+
+    def seg_desc(d):
+        return copy(seg_ref, SEGZ.at[z], seg_s.at[d - 1], seg_r.at[d - 1], along(d))
+
+    for d in (1, 2, 3):
+        seg_desc(d).start()
+    WK[own, :] = wk_ref[...]
+    WV[own, :] = wv_ref[...]
+    WQ[own, :] = wq_ref[...]
+    WU[own, :] = wu_ref[...]
+    turned = wo_ref[...].T
+    OWN_O[...] = turned
+    WO[own, :] = turned
+    turned = wd_ref[...].T
+    OWN_D[...] = turned
+    WD[own, :] = turned
+
+    def split_omega(h, carry):
+        om = om_ref[h]
+        hi = om.astype(BF)
+        low = (om - hi.astype(F32)).astype(BF)
+        zero = jnp.zeros((64, 256), BF)
+        OM1[h] = jnp.concatenate([hi, zero, hi, zero], axis=0)
+        OM2[h] = jnp.concatenate([low, zero], axis=0)
+        turned = jnp.concatenate([om, jnp.zeros((64, 256), F32)], axis=0).T
+        t_hi = turned.astype(BF)
+        t_low = (turned - t_hi.astype(F32)).astype(BF)
+        one_at = (lanes_of((256, 128)) == 64).astype(BF)
+        OMT[h] = jnp.concatenate([t_hi + one_at, t_low], axis=1)
+        return carry
+
+    lax.fori_loop(0, 3, split_omega, 0)
+
+    for s in range(2):
+        ag_pass(0, X, s)
+    w_pass(0)
+    w_pass(1)
+
+    for d in (1, 2, 3):
+        seg_desc(d).wait_recv()
+    seg_row = [seg_ref[s : s + 1, :] for s in range(2)]
+
+    def edge(s, side, dist):
+        if side == 0:
+            return SEGZ[(z + 4 - dist) % 4, s : s + 1, 255:256]
+        return SEGZ[(z + dist) % 4, s : s + 1, 0:1]
+
+    def reaches(side, dist):
+        return z >= dist if side == 0 else z + dist <= 3
+
+    for s in range(2):
+        wide = jnp.broadcast_to(seg_row[s].astype(F32), (256, 256))
+        col = wide.T
+        MSK[s] = (wide == col).astype(F32)
+        for side in range(2):
+            near = (col[:, 0:128] == edge(s, side, 1).astype(F32)).astype(F32)
+            CM[side, s] = jnp.where(reaches(side, 1), near, 0.0)
+
+    def first_row(s):
+        return (seg_row[s] == seg_row[s][:, 0:1]).astype(F32)
+
+    def last_row(s):
+        return (seg_row[s] == seg_row[s][:, 255:256]).astype(F32)
+
+    def project_keys(s):
+        rows = X[s]
+        made_k = nn(rows, WK[...]) * HEAD_DIM ** (-0.25)
+        made_v = nn(rows, WV[...])
+        zero = jnp.zeros((256, 64), F32)
+        lane = lanes_of((256, 128))
+        for h in range(3):
+            i = s * 3 + h
+            RK[i] = jnp.concatenate([made_k[:, 64 * h : 64 * h + 64], zero], axis=1)
+            v_h = jnp.concatenate([made_v[:, 64 * h : 64 * h + 64], zero], axis=1)
+            VX[i] = jnp.where((lane == 64) | (lane == 65), 1.0, v_h).astype(BF)
+
+    def project_queries(s):
+        made_q = nn(X[s], WQ[...]) * HEAD_DIM ** (-0.25)
+        zero = jnp.zeros((256, 64), F32)
+        for h in range(3):
+            RQ[s * 3 + h] = jnp.concatenate([made_q[:, 64 * h : 64 * h + 64], zero], axis=1)
+
+    def phi_of(scaled, h):
+        hi = scaled.astype(BF)
+        low = (scaled - hi.astype(F32)).astype(BF)
+        angles = nn(jnp.concatenate([hi, low], axis=1), OM1[h]) + nn(hi, OM2[h])
+        squares = 0.5 * jnp.sum(scaled * scaled, -1, keepdims=True)
+        return jnp.exp(angles - squares) * FEATS ** (-0.5)
+
+    def tables(ext, feats, s):
+        turned = ext.astype(F32).T[0:TAB, :]
+        both = jnp.concatenate([turned * first_row(s), turned * last_row(s)], axis=0)
+        return nn(both.astype(BF), feats)
+
+    def keys(s):
+        def body(h, carry):
+            i = s * 3 + h
+            phi = phi_of(RK[i], h)
+            PKF[i] = phi
+            low = phi.astype(BF)
+            PK[i] = low
+            made = tables(VX[i], low, s)
+            TBS[0, 1, i] = made[0:TAB].astype(BF)
+            TBS[0, 0, i] = made[TAB : 2 * TAB].astype(BF)
+            return carry
+
+        lax.fori_loop(0, 3, body, 0)
+
+    def queries(s):
+        def body(h, carry):
+            i = s * 3 + h
+            phi = phi_of(RQ[i], h)
+            PQF[i] = phi
+            low = phi.astype(BF)
+            PQ[i] = low
+            score = jnp.where(MSK[s] > 0, nt(low, PK[i]), 0.0).astype(BF)
+            SS[i] = score
+            MIX[i] = nn(score, VX[i])
+            return carry
+
+        lax.fori_loop(0, 3, body, 0)
+
+    def mixing(s):
+        tb_take(0, s, COMB)
+
+        def body(h, carry):
+            i = s * 3 + h
+            cross = nt(PQ[i], COMB[i])
+            numer = MIX[i] + jnp.where(CM[0, s] > 0, cross[:, 0:128], 0.0)
+            numer = numer + jnp.where(CM[1, s] > 0, cross[:, 128:256], 0.0)
+            denom = numer[:, 64:65]
+            mixed = numer / denom
+            MIX[i] = jnp.where(lanes_of((256, 128)) < 64, mixed, 0.0)
+            DEN[i] = jnp.broadcast_to(denom, (256, 128))
+            return carry
+
+        lax.fori_loop(0, 3, body, 0)
+        MIXC[s] = jnp.concatenate(
+            [MIX[s * 3][:, 0:64], MIX[s * 3 + 1][:, 0:64], MIX[s * 3 + 2][:, 0:64]], axis=1
+        ).astype(BF)
+
+    def tb_desc(way, s, side, dist):
+        heads = pl.ds(s * 3, 3)
+        return copy(
+            TBS.at[way, side, heads],
+            TBR.at[way, side, dist - 1, heads],
+            tb_s.at[way, s, side, dist - 1],
+            tb_r.at[way, s, side, dist - 1],
+            along(dist if side == 0 else 4 - dist),
+        )
+
+    def tb_each(act):
+        for side in range(2):
+            for dist in (1, 2):
+
+                @pl.when(reaches(1 - side, dist))
+                def _():
+                    act(side, dist)
+
+    def tb_send(way, s):
+        tb_each(lambda side, dist: tb_desc(way, s, side, dist).start())
+
+    def tb_take(way, s, comb):
+        for side in range(2):
+            for dist in (1, 2):
+
+                @pl.when(reaches(side, dist))
+                def _():
+                    tb_desc(way, s, side, dist).wait_recv()
+
+            both = (edge(s, side, 1) == edge(s, side, 2)) & reaches(side, 2)
+            both = jnp.broadcast_to(both, (TAB, 256))
+            for h in range(3):
+                i = s * 3 + h
+                near = TBR[way, side, 0, i].astype(F32)
+                total = near + jnp.where(both, TBR[way, side, 1, i].astype(F32), 0.0)
+                comb[i, 128 * side : 128 * side + TAB, :] = total.astype(BF)
+
+    def attn_out(s):
+        P[s] = nt(MIXC[s], WO[...])
+
+    gain_attn, shift_attn, gain_ffn, shift_ffn, bias_down = (
+        ref[...].reshape(1, 768) for ref in (ga_ref, sa_ref, gf_ref, sf_ref, bd_ref)
+    )
+    ARS[0] = jnp.zeros((8, 768), F32)
+
+    def add_small(row, value):
+        ARS[0, row : row + 1, :] = ARS[0, row : row + 1, :] + value
+
+    def over_rows(value):
+        return jnp.sum(value, 0, keepdims=True)
+
+    def norm_one(s, attn):
+        normed, inv_std = norm_stats(x_ref[s].astype(F32) + attn)
+        first = normed * gain_attn + shift_attn
+        NORM1[s], FIRST[s] = normed, first
+        INV1[s] = jnp.broadcast_to(inv_std, (64, 128))
+        FI[s, chunk(t), :] = first.astype(BF)
+
+    def norm_two(s, branch):
+        normed, inv_std = norm_stats(FIRST[s] + branch + bias_down)
+        out_ref[s] = (normed * gain_ffn + shift_ffn).astype(BF)
+        cot = cot_ref[s].astype(F32)
+        grad = norm_grad(cot, normed, inv_std, gain_ffn)
+        GH2[s] = grad
+        G2[s, chunk(t), :] = grad.astype(BF)
+        add_small(2, over_rows(cot * normed))
+        add_small(3, over_rows(cot))
+        add_small(4, over_rows(grad))
+
+    def norm_one_back(s, summed):
+        grad_first = GH2[s] + summed
+        normed = NORM1[s]
+        grad = norm_grad(grad_first, normed, INV1[s][:, 0:1], gain_attn)
+        GH1[s] = grad
+        G1[s, chunk(t), :] = grad.astype(BF)
+        add_small(0, over_rows(grad_first * normed))
+        add_small(1, over_rows(grad_first))
+
+    def tile(j):
+        return pl.ds(pl.multiple_of(j * 256, 256), 256)
+
+    def ffn_up(s):
+        def body(j, carry):
+            upper = nn(FI[s], WU[:, tile(j)]) + bu_ref[tile(j)].reshape(1, 256)
+            cdf = 0.5 * (1.0 + lax.erf(upper * root_half))
+            HID[s, :, tile(j)] = (upper * cdf).astype(BF)
+            SLOPE[s, :, tile(j)] = cdf + upper * inv_root_tau * jnp.exp(-0.5 * upper * upper)
+            return carry
+
+        lax.fori_loop(0, 3, body, 0)
+
+    def ffn_down(s):
+        def body(j, carry):
+            P[s, :, tile(j)] = nt(HID[s], WD[tile(j), :])
+            return carry
+
+        lax.fori_loop(0, 3, body, 0)
+
+    def ffn_back_hidden(s):
+        def body(j, carry):
+            grad = (nn(G2[s], WD[:, tile(j)]) * SLOPE[s, :, tile(j)]).astype(BF)
+            GUP[s, :, tile(j)] = grad
+            ARS[0, 5:6, tile(j)] = ARS[0, 5:6, tile(j)] + over_rows(grad.astype(F32))
+            return carry
+
+        lax.fori_loop(0, 3, body, 0)
+
+    def ffn_back_rows(s):
+        def body(j, carry):
+            P[s, :, tile(j)] = nt(GUP[s], WU[tile(j), :])
+            return carry
+
+        lax.fori_loop(0, 3, body, 0)
+
+    def slots(i):
+        narrow, wide = (GON, YSN, YRN, ZSN, ZRN), (GOW, YSW, YRW, ZSW, ZRW)
+        return [ref.at[i] for ref in narrow] if i < 4 else [ref.at[i - 4] for ref in wide]
+
+    def half_lanes(yy, j):
+        return pl.ds(pl.multiple_of(yy * 384 + j * 128, 128), 128)
+
+    def weight_grad(i, left, right):
+        own_half, sent = slots(i)[0], slots(i)[1]
+
+        def made(yy, j):
+            lanes = half_lanes(yy, j)
+            return tn(left[0, :, lanes], right[0]) + tn(left[1, :, lanes], right[1])
+
+        def rows(j):
+            return pl.ds(pl.multiple_of(j * 128, 128), 128)
+
+        def other(j, carry):
+            sent[rows(j), :] = made(1 - y, j).astype(BF)
+            return carry
+
+        def here(j, carry):
+            own_half[rows(j), :] = made(y, j)
+            return carry
+
+        lax.fori_loop(0, 3, other, 0)
+        for n in range(4):
+            block = (z + (2, 1, 3, 0)[n]) % 4 if i < 4 else n + (1 - z // 2) * (3 - 2 * n)
+            gy_desc(i, block).start()
+        lax.fori_loop(0, 3, here, 0)
+
+    def z_rows(block):
+        return pl.ds(pl.multiple_of(block * 96, 96), 96)
+
+    def gy_desc(i, block):
+        sent, came_y = slots(i)[1:3]
+        return copy(sent.at[z_rows(block), :], came_y.at[block], gy_s.at[i, block], gy_r.at[i, block], yp)
+
+    def gz_desc(i, d):
+        sent, came_z = slots(i)[3:5]
+        return copy(sent.at[d - 1], came_z.at[d - 1], gz_s.at[i, d - 1], gz_r.at[i, d - 1], along(d))
+
+    def chip_sum(i, block):
+        own_half, _, came_y, _, _ = slots(i)
+        gy_desc(i, block).wait_recv()
+        return own_half[z_rows(block), :] + came_y[block].astype(F32)
+
+    def g_pass(i):
+        sent = slots(i)[3]
+        for d in (2, 1, 3):
+            sent[d - 1] = chip_sum(i, (z + d) % 4).astype(BF)
+            gz_desc(i, d).start()
+
+    def gc_desc(i, way, e):
+        sent, came_z = ZSW.at[i - 4, way, e], ZRW.at[i - 4, way, e]
+        return copy(sent, came_z, gc_s.at[i - 4, way, e], gc_r.at[i - 4, way, e], along(4 + step_of(way)))
+
+    def gives(way, e):
+        return z + e < 3 if way == 0 else z > e
+
+    def behind(way):
+        return z > 0 if way == 0 else z < 3
+
+    def g_relay(i, e):
+        for way in range(2):
+
+            @pl.when(gives(way, e))
+            def _():
+                total = chip_sum(i, (z + 4 + (e + 1) * step_of(way)) % 4)
+                ZSW[i - 4, way, e] = total.astype(BF)
+                if e < 2:
+
+                    @pl.when(behind(way))
+                    def _():
+                        gc_desc(i, way, e + 1).wait_recv()
+                        ZSW[i - 4, way, e] = (total + ZRW[i - 4, way, e + 1].astype(F32)).astype(BF)
+
+                gc_desc(i, way, e).start()
+
+    def g_last(i, out):
+        total = chip_sum(i, z)
+        if i < 4:
+            arrived = slots(i)[4]
+            for d in (1, 2, 3):
+                gz_desc(i, d).wait_recv()
+                total = total + arrived[d - 1].astype(F32)
+            out[...] = total
+            return
+        out[...] = total
+        for way in range(2):
+
+            @pl.when(behind(way))
+            def _():
+                gc_desc(i, way, 0).wait_recv()
+                out[...] = out[...] + ZRW[i - 4, way, 0].astype(F32)
+
+    def ar_desc(stage):
+        where = (sib, far, yp)[stage]
+        return copy(ARS.at[stage], ARR.at[stage], ar_s.at[stage], ar_r.at[stage], where)
+
+    def ar_take(stage):
+        ar_desc(stage).wait_recv()
+        came = ARR[stage]
+        if stage < 2:
+            rows = lax.broadcasted_iota(jnp.int32, (8, 768), 0)
+            came = jnp.where(rows < 5, came, 0.0)
+        ARS[stage + 1] = ARS[stage] + came
+
+    def ar_z_desc(i):
+        return copy(ARS.at[3], ARZ.at[z], ar_s.at[3 + i], ar_r.at[3 + i], along(1 + i))
+
+    def ar_z_start():
+        ARZ[z] = ARS[3]
+        for i in range(3):
+            ar_z_desc(i).start()
+
+    def ar_z_take():
+        for i in range(3):
+            ar_z_desc(i).wait_recv()
+        small_ref[...] = (ARZ[0] + ARZ[1]) + (ARZ[2] + ARZ[3])
+
+    def grad_tables(s):
+        GM[...] = nn(G1[s], WO[...])
+        lane = lanes_of((256, 128))
+        zero = jnp.zeros((256, 64), F32)
+        for h in range(3):
+            i = s * 3 + h
+            gm = jnp.concatenate([GM[:, 64 * h : 64 * h + 64], zero], axis=1)
+            denom = DEN[i]
+            slope = -jnp.sum(gm * MIX[i], -1, keepdims=True) / denom
+            s_hi = slope.astype(BF).astype(F32)
+            ext = jnp.where(lane == 64, s_hi, gm / denom)
+            GX[i] = jnp.where(lane == 65, slope - s_hi, ext).astype(BF)
+
+        def body(h, carry):
+            i = s * 3 + h
+            made = tables(GX[i], PQ[i], s)
+            TBS[1, 1, i] = made[0:TAB].astype(BF)
+            TBS[1, 0, i] = made[TAB : 2 * TAB].astype(BF)
+            return carry
+
+        lax.fori_loop(0, 3, body, 0)
+
+    def pair(ext, s):
+        ext = ext.astype(F32)
+        return jnp.concatenate([ext * CM[0, s], ext * CM[1, s]], axis=1).astype(BF)
+
+    def through_phi(grad_phi, phi, scaled, h):
+        both = nn((grad_phi * phi).astype(BF), OMT[h])
+        both = both[:, 0:128] + both[:, 128:256]
+        return (both - scaled * both[:, 64:65]) * HEAD_DIM ** (-0.25)
+
+    def side_by_side(heads):
+        return jnp.concatenate([heads[h][:, 0:64] for h in range(3)], axis=1).astype(BF)
+
+    def back_queries(s):
+        def body(h, carry):
+            i = s * 3 + h
+            ext = GX[i]
+            pairs = jnp.where(MSK[s] > 0, nt(ext, VX[i]), 0.0).astype(BF)
+            grad = nn(pairs, PK[i]) + nn(pair(ext, s), COMB[i])
+            GM3[h] = through_phi(grad, PQF[i], RQ[i], h)
+            GKL[i] = tn(pairs, PQ[i])
+            GVL[i] = tn(SS[i], ext)
+            return carry
+
+        lax.fori_loop(0, 3, body, 0)
+        RGQ[s] = side_by_side(GM3)
+
+    def back_keys(s):
+        tb_take(1, s, GCOMB)
+
+        def body(h, carry):
+            i = s * 3 + h
+            grad = GKL[i] + nn(pair(VX[i], s), GCOMB[i])
+            GM3[h] = through_phi(grad, PKF[i], RK[i], h)
+            cross = nt(PK[i], GCOMB[i])
+            gv = GVL[i] + jnp.where(CM[0, s] > 0, cross[:, 0:128], 0.0)
+            GV3[h] = gv + jnp.where(CM[1, s] > 0, cross[:, 128:256], 0.0)
+            return carry
+
+        lax.fori_loop(0, 3, body, 0)
+        RGK[s] = side_by_side(GM3)
+        RGV[s] = side_by_side(GV3)
+
+    def input_rows(s):
+        def body(j, carry):
+            made = nt(RGQ[s], WQ[tile(j), :]) + nt(RGK[s], WK[tile(j), :])
+            P[s, :, tile(j)] = made + nt(RGV[s], WV[tile(j), :])
+            return carry
+
+        lax.fori_loop(0, 3, body, 0)
+
+    w_send(3)
+    w_send(4)
+    w_pass(2)
+    w_wait(0)
+    w_wait(1)
+    ag_wait(0, X, 0)
+    project_keys(0)
+    keys(0)
+    tb_send(0, 0)
+    w_relay(4, 0)
+    w_pass(3)
+    ag_wait(0, X, 1)
+    project_keys(1)
+    keys(1)
+    tb_send(0, 1)
+    w_relay(4, 1)
+    w_wait(2)
+    project_queries(0)
+    queries(0)
+    w_relay(4, 2)
+    project_queries(1)
+    queries(1)
+    w_send(5)
+    mixing(0)
+    w_wait(3)
+    attn_out(0)
+    rs_start(0, 0)
+    mixing(1)
+    attn_out(1)
+    rs_start(0, 1)
+    rs_mid(0, 0)
+    rs_mid(0, 1)
+    w_relay(5, 0)
+    norm_one(0, rs_fin(0, 0))
+    ag_start(1, FI, 0)
+    norm_one(1, rs_fin(0, 1))
+    ag_start(1, FI, 1)
+    w_relay(5, 1)
+    ag_pass(1, FI, 0)
+    ag_pass(1, FI, 1)
+    w_relay(5, 2)
+    ag_wait(1, FI, 0)
+    w_wait(4)
+    ffn_up(0)
+    w_wait(5)
+    ffn_down(0)
+    rs_start(1, 0)
+    ag_wait(1, FI, 1)
+    ffn_up(1)
+    rs_mid(1, 0)
+    ffn_down(1)
+    rs_start(1, 1)
+    norm_two(0, rs_fin(1, 0))
+    ag_start(2, G2, 0)
+    rs_mid(1, 1)
+    norm_two(1, rs_fin(1, 1))
+    ag_start(2, G2, 1)
+    ag_pass(2, G2, 0)
+    ag_pass(2, G2, 1)
+    ag_wait(2, G2, 0)
+    ffn_back_hidden(0)
+    ffn_back_rows(0)
+    rs_start(2, 0)
+    ag_wait(2, G2, 1)
+    ffn_back_hidden(1)
+    rs_mid(2, 0)
+    ffn_back_rows(1)
+    rs_start(2, 1)
+    weight_grad(5, G2, HID)
+    rs_mid(2, 1)
+    norm_one_back(0, rs_fin(2, 0))
+    ag_start(3, G1, 0)
+    norm_one_back(1, rs_fin(2, 1))
+    ag_start(3, G1, 1)
+    ar_desc(0).start()
+    weight_grad(4, FI, GUP)
+    ag_pass(3, G1, 0)
+    g_relay(5, 2)
+    ag_pass(3, G1, 1)
+    ar_take(0)
+    ar_desc(1).start()
+    ag_wait(3, G1, 0)
+    grad_tables(0)
+    tb_send(1, 0)
+    ag_wait(3, G1, 1)
+    grad_tables(1)
+    tb_send(1, 1)
+    weight_grad(3, G1, MIXC)
+    g_relay(5, 1)
+    ar_take(1)
+    ar_desc(2).start()
+    back_queries(0)
+    g_relay(5, 0)
+    back_queries(1)
+    weight_grad(2, X, RGQ)
+    g_relay(4, 2)
+    ar_take(2)
+    ar_z_start()
+    back_keys(0)
+    g_relay(4, 1)
+    input_rows(0)
+    rs_start(3, 0)
+    back_keys(1)
+    rs_mid(3, 0)
+    weight_grad(0, X, RGK)
+    weight_grad(1, X, RGV)
+    g_relay(4, 0)
+    input_rows(1)
+    rs_start(3, 1)
+    g_pass(3)
+    g_pass(2)
+    rs_mid(3, 1)
+    g_pass(0)
+    g_pass(1)
+    gin_ref[0] = (GH1[0] + rs_fin(3, 0)).astype(BF)
+    gin_ref[1] = (GH1[1] + rs_fin(3, 1)).astype(BF)
+    ar_z_take()
+    g_last(5, od_ref)
+    g_last(4, ou_ref)
+    g_last(3, oo_ref)
+    g_last(2, oq_ref)
+    g_last(0, ok_ref)
+    g_last(1, ov_ref)
+
+    for s in range(2):
+        for op, buf in enumerate((X, FI, G2, G1)):
+            for which in range(3):
+                ag_desc(op, buf, s, which).wait_send()
+        for op in range(4):
+            sib_desc(op, s, 0).wait_send()
+            sib_desc(op, s, 1).wait_send()
+            xrs_desc(op, s).wait_send()
+        for way in range(2):
+            tb_each(lambda side, dist: tb_desc(way, s, side, dist).wait_send())
+    for i in range(6):
+        wy_desc(i, 0).wait_send()
+        for block in range(4):
+            gy_desc(i, block).wait_send()
+        for d in (1, 2, 3):
+            if i < 4:
+                wy_desc(i, d).wait_send()
+                wz_desc(i, d).wait_send()
+                gz_desc(i, d).wait_send()
+    for i in (4, 5):
+        for way in range(2):
+            for j in range(3):
+
+                @pl.when(goes(way, j))
+                def _():
+                    wc_desc(i, way, j).wait_send()
+
+                @pl.when(came(way, j))
+                def _():
+                    wf_desc(i, way, j).wait_send()
+
+                @pl.when(gives(way, j))
+                def _():
+                    gc_desc(i, way, j).wait_send()
+
+    for stage in range(3):
+        ar_desc(stage).wait_send()
+        ar_z_desc(stage).wait_send()
+        seg_desc(stage + 1).wait_send()
+
+
+def hand_out(
+    out_ref, gin_ref, ok_ref, ov_ref, oq_ref, oo_ref, ou_ref, od_ref, small_ref,
+    out_o, gin_o, q_o, k_o, v_o, o_o, ga_o, sa_o, u_o, bu_o, d_o, bd_o, gf_o, sf_o,
+):
+    pairs = ((out_o, out_ref), (gin_o, gin_ref), (q_o, oq_ref), (k_o, ok_ref), (v_o, ov_ref), (u_o, ou_ref))
+    for dst, src in pairs:
+        dst[...] = src[...]
+    o_o[...] = oo_ref[...].T
+    d_o[...] = od_ref[...].T
+    for row, dst in enumerate((ga_o, sa_o, gf_o, sf_o, bd_o, bu_o)):
+        dst[...] = small_ref[row, :]
+
+
+def dma(*shape):
+    return pltpu.SemaphoreType.DMA(shape)
+
+
+def fast_device(
+    inputs, seg_ids, feature_map, w_query, w_key, w_value, w_out, gain_attn, shift_attn,
+    w_up, bias_up, w_down, bias_down, gain_ffn, shift_ffn, cotangent,
+):
+    vm = pltpu.VMEM
+    scratch = [
+        vm((2, 256, 768), BF), vm((2, 256, 768), BF), vm((2, 256, 768), BF), vm((2, 256, 768), BF),
+        vm((768, 192), BF), vm((768, 192), BF), vm((768, 192), BF), vm((768, 192), BF),
+        vm((768, 768), BF), vm((768, 768), BF), vm((96, 192), BF), vm((96, 768), BF),
+        vm((2, 256, 768), F32), vm((2, 256, 768), BF), vm((2, 256, 768), F32), vm((2, 256, 768), BF),
+        vm((2, 64, 768), F32), vm((2, 64, 768), F32), vm((2, 64, 128), F32),
+        vm((2, 64, 768), F32), vm((2, 64, 768), F32),
+        vm((6, 256, 128), F32), vm((6, 256, 128), F32), vm((6, 256, 128), BF),
+        vm((6, 256, 256), F32), vm((6, 256, 256), F32), vm((6, 256, 256), BF), vm((6, 256, 256), BF),
+        vm((6, 256, 256), BF),
+        vm((2, 256, 256), F32), vm((2, 2, 256, 128), F32), vm((4, 2, 256), jnp.int32),
+        vm((3, 256, 256), BF), vm((3, 128, 256), BF), vm((3, 256, 256), BF),
+        vm((6, 256, 128), F32), vm((6, 256, 128), F32), vm((6, 256, 128), BF),
+        vm((6, 256, 256), F32), vm((6, 256, 128), F32),
+        vm((256, 192), F32), vm((3, 256, 128), F32), vm((3, 256, 128), F32),
+        vm((2, 256, 192), BF), vm((2, 256, 192), BF), vm((2, 256, 192), BF), vm((2, 256, 192), BF),
+        vm((2, 2, 6, TAB, 256), BF), vm((2, 2, 2, 6, TAB, 256), BF), vm((6, 256, 256), BF), vm((6, 256, 256), BF),
+        vm((4, 2, 2, 64, 768), BF), vm((4, 2, 2, 64, 768), BF), vm((4, 2, 64, 768), BF), vm((4, 2, 64, 768), BF),
+        vm((4, 384, 192), F32), vm((2, 384, 768), F32),
+        vm((4, 384, 192), BF), vm((2, 384, 768), BF),
+        vm((4, 4, 96, 192), BF), vm((2, 4, 96, 768), BF),
+        vm((4, 3, 96, 192), BF), vm((2, 2, 3, 96, 768), BF),
+        vm((4, 3, 96, 192), BF), vm((2, 2, 3, 96, 768), BF),
+        vm((4, 8, 768), F32), vm((3, 8, 768), F32), vm((4, 8, 768), F32),
+        dma(4, 2, 3), dma(4, 2, 3), dma(4, 2, 3), dma(4, 2, 3), dma(3), dma(3),
+        dma(4, 3), dma(4, 3), dma(6, 4), dma(6, 4), dma(2, 2, 3), dma(2, 2, 3), dma(2, 2, 3), dma(2, 2, 3),
+        dma(6, 4), dma(6, 4), dma(4, 3), dma(4, 3), dma(2, 2, 3), dma(2, 2, 3),
+        dma(2, 2, 2, 2), dma(2, 2, 2, 2), dma(6), dma(6),
+    ]
+    in_vmem = pl.BlockSpec(memory_space=pltpu.VMEM)
+    shape = jax.ShapeDtypeStruct
+    narrow, wide, rows, vec = shape((96, 192), F32), shape((96, 768), F32), shape((2, 64, 768), BF), shape((768,), F32)
+    made = pl.pallas_call(
+        layer_kernel,
+        out_shape=(rows, rows, narrow, narrow, narrow, narrow, wide, wide, shape((8, 768), F32)),
+        in_specs=[in_vmem] * 16,
+        out_specs=(in_vmem,) * 9,
+        scratch_shapes=scratch,
+        compiler_params=pltpu.CompilerParams(
+            collective_id=0, has_side_effects=True, vmem_limit_bytes=67043328
+        ),
+    )(
+        inputs, seg_ids, feature_map, w_query, w_key, w_value, w_out, gain_attn, shift_attn,
+        w_up, bias_up, w_down, bias_down, gain_ffn, shift_ffn, cotangent,
+    )
+    return pl.pallas_call(
+        hand_out,
+        out_shape=(
+            rows, rows, narrow, narrow, narrow, shape((192, 96), F32), vec, vec,
+            wide, vec, shape((768, 96), F32), vec, vec, vec,
+        ),
+        in_specs=[in_vmem] * 9,
+        out_specs=(in_vmem,) * 14,
+    )(*made)
+
+
 def solution(mesh):
     placed = (
         P("shard", ("ctx", "tp"), None),
@@ -347,8 +1255,9 @@
         P(),
         P("shard", ("ctx", "tp"), None),
     )
+    sizes = tuple(mesh.shape[axis] for axis in ("shard", "ctx", "tp"))
     return jax.shard_map(
-        per_device,
+        fast_device if sizes == (2, 4, 4) else per_device,
         mesh=mesh,
         in_specs=placed,
         out_specs=(

time: 1020 us -> 164 us (0.16)
  waiting for transfers between devices: 500 us -> 0 us
  blocking collectives: 320 us -> 0 us
  Pallas kernels: 0 us -> 160 us
  local copies, waits for them, and re-layouts: 85.6 us -> 3.59 us
  matrix products: 73.6 us -> 0 us
  between operations: 16.6 us -> 0.66 us
  other arithmetic: 13 us -> 0 us
    reduce_scatter x6 -> x0, waiting for transfers between devices: 225 us -> none  [the longest x1 73.1 us: per_device(): lax.psum_scatter(grad_up, ('shard', 'ctx'), scatter_dimension=0, tiled=True)]
    unnamed x17 -> x0, waiting for transfers between devices: 197 us -> none
    all_gather x8 -> x0, blocking collectives: 163 us -> none  [the longest x1 32.5 us: per_device(): lax.all_gather(w_key, ('shard', 'ctx'), axis=0, tiled=True)]
    pallas_call x0 -> x2, Pallas kernels: none -> 160 us  [the longest x1 157 us: fast_device(): pl.pallas_call(layer_kernel, out_shape=(rows, rows, narrow, narrow, narro...]
    psum x3 -> x0, blocking collectives: 157 us -> none  [the longest x1 96.2 us: per_device(): kv_sum, z_sum = lax.psum((kv_part, z_part), 'ctx')]
    dot_general x38 -> x0, matrix products: 72.3 us -> none  [the longest x4 10.2 us: segment_apply(): jnp.einsum('chx,hxe->che', spread_rows(mask_low, left), table, preferred_...]
    mul x48 -> x0, local copies, waits for them, and re-layouts: 51.9 us -> none  [the longest x40 51.8 us: spread_rows(): wide = mask_low[:, None, :, None] * left[:, :, None, :]]
    all_gather x2 -> x0, waiting for transfers between devices: 44.3 us -> none  [the longest x1 38.5 us: per_device(): lax.all_gather(w_down, ('shard', 'ctx'), axis=1, tiled=True)]
  transfers between devices with their start and end apart: 13 -> 0, of which waited for: 11 -> 0; matrix products, arithmetic and copies ran while one was open for 7% -> 0% of each run, Pallas kernels for 0% -> 0%
where the time goes in v1:
time: 164 us
  Pallas kernels  160 us (98%)
  local copies, waits for them, and re-layouts  3.59 us (2%)
    pallas_call x1, Pallas kernels, fast_device(): pl.pallas_call(layer_kernel, out_shape=(rows, rows, narrow, narrow, narro...  157 us

profile of v1, /device:TPU:0, one launch (start us, length us, event | category | flops | bytes accessed | tf_op | source)
XLA Modules:
  0.0 164.1 jit_solution(15124195122452371583)
XLA Ops:
  0.6 1.7 %copy.30.wd_ref = bf16[768,96]{1,0:T(8,128)(2,1)} copy(bf16[768,96]{0,1:T(8,128)(2,1)} %param.27) | data formatting | bytes 294912 | tf_op args[11]
  2.4 157.2 %shard_map.263 = (bf16[2,64,768]{2,1,0:T(8,128)(2,1)}, bf16[2,64,768]{2,1,0:T(8,128)(2,1)}, f32[96,192]{1,0:T(8,128)}, f32[96,192]{1,0:T(8,128)}, f32[96,192]{1,...) custom-call(bf16[2,64,768]{2,1,0:T(8,128)(2,1)} %x_ref.1, ...), custom_call_target="tpu_custom_call" | custom-call | tf_op jit(solution)/shard_map/pallas_call | solution.py:1215
  159.6 2.6 %shard_map.264 = (bf16[2,64,768]{2,1,0:T(8,128)(2,1)}, bf16[2,64,768]{2,1,0:T(8,128)(2,1)}, f32[96,192]{1,0:T(8,128)}, f32[96,192]{1,0:T(8,128)}, f32[96,192]{1,...) custom-call(bf16[2,64,768]{2,1,0:T(8,128)(2,1)} %get-tuple-element.2, ...), custom_call_target="tpu_custom_call" | custom-call | tf_op jit(solution)/shard_map/pallas_call | solution.py:1228
  162.2 1.9 %copy.31 = f32[768,96]{0,1:T(8,128)} copy(f32[768,96]{1,0:T(8,128)} %get-tuple-element.42) | data formatting | bytes 589824 | tf_op jit(solution)/shard_map/pallas_call | solution.py:1228

commit v2 on v1

--- a/solution.py
+++ b/solution.py
@@ -372,7 +372,7 @@
     x_ref, seg_ref, om_ref, wq_ref, wk_ref, wv_ref, wo_ref, ga_ref, sa_ref, wu_ref, bu_ref, wd_ref,
     bd_ref, gf_ref, sf_ref, cot_ref,
     out_ref, gin_ref, ok_ref, ov_ref, oq_ref, oo_ref, ou_ref, od_ref, small_ref,
-    X, FI, G2, G1, WK, WV, WQ, WO, WU, WD, OWN_O, OWN_D, P, HID, SLOPE, GUP,
+    X, FI, G2, G1, WK, WV, WQ, WO, WU, WD, OWN_O, P, HID, SLOPE, GUP,
     FIRST, NORM1, INV1, GH2, GH1,
     RQ, RK, VX, PQF, PKF, PQ, PK, SS, MSK, CM, SEGZ,
     OM1, OM2, OMT,
@@ -459,7 +459,7 @@
         return kept + XR[op, s].astype(F32)
 
     gathered = (WK, WV, WQ, WO, WU, WD)
-    mine = (wk_ref, wv_ref, wq_ref, OWN_O, wu_ref, OWN_D)
+    mine = (wk_ref, wv_ref, wq_ref, OWN_O, wu_ref, wd_ref)
 
     def wz_desc(i, d):
         dst = gathered[i].at[block_rows(y, z), :]
@@ -498,6 +498,7 @@
                 def _():
                     wc_desc(i, way, 0).start()
 
+    def w_over(i):
         wy_desc(i, 0).start()
 
     def w_pass(i):
@@ -535,13 +536,15 @@
                 def _():
                     wf_desc(i, way, j).wait_recv()
 
-    w_send(0)
-    w_send(1)
+    for i in range(2):
+        w_send(i)
+        w_over(i)
     own = block_rows(y, z)
     for s in range(2):
         X[s, chunk(t), :] = x_ref[s]
         ag_start(0, X, s)
     w_send(2)
+    w_over(2)
     TBR[...] = jnp.zeros_like(TBR)
     COMB[...] = jnp.zeros_like(COMB)
     GCOMB[...] = jnp.zeros_like(GCOMB)
@@ -558,9 +561,7 @@
     turned = wo_ref[...].T
     OWN_O[...] = turned
     WO[own, :] = turned
-    turned = wd_ref[...].T
-    OWN_D[...] = turned
-    WD[own, :] = turned
+    WD[own, :] = wd_ref[...]
 
     def split_omega(h, carry):
         om = om_ref[h]
@@ -651,7 +652,7 @@
             TBS[0, 0, i] = made[TAB : 2 * TAB].astype(BF)
             return carry
 
-        lax.fori_loop(0, 3, body, 0)
+        lax.fori_loop(0, 3, body, 0, unroll=True)
 
     def queries(s):
         def body(h, carry):
@@ -665,7 +666,7 @@
             MIX[i] = nn(score, VX[i])
             return carry
 
-        lax.fori_loop(0, 3, body, 0)
+        lax.fori_loop(0, 3, body, 0, unroll=True)
 
     def mixing(s):
         tb_take(0, s, COMB)
@@ -681,39 +682,46 @@
             DEN[i] = jnp.broadcast_to(denom, (256, 128))
             return carry
 
-        lax.fori_loop(0, 3, body, 0)
+        lax.fori_loop(0, 3, body, 0, unroll=True)
         MIXC[s] = jnp.concatenate(
             [MIX[s * 3][:, 0:64], MIX[s * 3 + 1][:, 0:64], MIX[s * 3 + 2][:, 0:64]], axis=1
         ).astype(BF)
 
     def tb_desc(way, s, side, dist):
         heads = pl.ds(s * 3, 3)
+        src = TBS.at[way, side, heads] if dist == 1 else TBR.at[way, side, 0, heads]
         return copy(
-            TBS.at[way, side, heads],
+            src,
             TBR.at[way, side, dist - 1, heads],
             tb_s.at[way, s, side, dist - 1],
             tb_r.at[way, s, side, dist - 1],
-            along(dist if side == 0 else 4 - dist),
+            along(1 if side == 0 else 3),
         )
 
-    def tb_each(act):
+    def tb_send(way, s):
         for side in range(2):
-            for dist in (1, 2):
-
-                @pl.when(reaches(1 - side, dist))
-                def _():
-                    act(side, dist)
-
-    def tb_send(way, s):
-        tb_each(lambda side, dist: tb_desc(way, s, side, dist).start())
+
+            @pl.when(reaches(1 - side, 1))
+            def _():
+                tb_desc(way, s, side, 1).start()
+
+    def tb_relay(way, s):
+        for side in range(2):
+
+            @pl.when(reaches(side, 1))
+            def _():
+                tb_desc(way, s, side, 1).wait_recv()
+
+            @pl.when((z == 1) | (z == 2))
+            def _():
+                tb_desc(way, s, side, 2).start()
 
     def tb_take(way, s, comb):
         for side in range(2):
-            for dist in (1, 2):
-
-                @pl.when(reaches(side, dist))
-                def _():
-                    tb_desc(way, s, side, dist).wait_recv()
+
+            @pl.when(reaches(side, 2))
+            def _():
+                tb_desc(way, s, side, 2).wait_recv()
 
             both = (edge(s, side, 1) == edge(s, side, 2)) & reaches(side, 2)
             both = jnp.broadcast_to(both, (TAB, 256))
@@ -775,14 +783,14 @@
             SLOPE[s, :, tile(j)] = cdf + upper * inv_root_tau * jnp.exp(-0.5 * upper * upper)
             return carry
 
-        lax.fori_loop(0, 3, body, 0)
+        lax.fori_loop(0, 3, body, 0, unroll=True)
 
     def ffn_down(s):
         def body(j, carry):
             P[s, :, tile(j)] = nt(HID[s], WD[tile(j), :])
             return carry
 
-        lax.fori_loop(0, 3, body, 0)
+        lax.fori_loop(0, 3, body, 0, unroll=True)
 
     def ffn_back_hidden(s):
         def body(j, carry):
@@ -791,14 +799,14 @@
             ARS[0, 5:6, tile(j)] = ARS[0, 5:6, tile(j)] + over_rows(grad.astype(F32))
             return carry
 
-        lax.fori_loop(0, 3, body, 0)
+        lax.fori_loop(0, 3, body, 0, unroll=True)
 
     def ffn_back_rows(s):
         def body(j, carry):
             P[s, :, tile(j)] = nt(GUP[s], WU[tile(j), :])
             return carry
 
-        lax.fori_loop(0, 3, body, 0)
+        lax.fori_loop(0, 3, body, 0, unroll=True)
 
     def slots(i):
         narrow, wide = (GON, YSN, YRN, ZSN, ZRN), (GOW, YSW, YRW, ZSW, ZRW)
@@ -807,28 +815,32 @@
     def half_lanes(yy, j):
         return pl.ds(pl.multiple_of(yy * 384 + j * 128, 128), 128)
 
-    def weight_grad(i, left, right):
-        own_half, sent = slots(i)[0], slots(i)[1]
-
-        def made(yy, j):
-            lanes = half_lanes(yy, j)
-            return tn(left[0, :, lanes], right[0]) + tn(left[1, :, lanes], right[1])
-
-        def rows(j):
-            return pl.ds(pl.multiple_of(j * 128, 128), 128)
+    def weight_part(left, right, yy, j):
+        lanes = half_lanes(yy, j)
+        return tn(left[0, :, lanes], right[0]) + tn(left[1, :, lanes], right[1])
+
+    def half_rows(j):
+        return pl.ds(pl.multiple_of(j * 128, 128), 128)
+
+    def weight_send(i, left, right):
+        sent = slots(i)[1]
 
         def other(j, carry):
-            sent[rows(j), :] = made(1 - y, j).astype(BF)
-            return carry
-
-        def here(j, carry):
-            own_half[rows(j), :] = made(y, j)
+            sent[half_rows(j), :] = weight_part(left, right, 1 - y, j).astype(BF)
             return carry
 
         lax.fori_loop(0, 3, other, 0)
         for n in range(4):
             block = (z + (2, 1, 3, 0)[n]) % 4 if i < 4 else n + (1 - z // 2) * (3 - 2 * n)
             gy_desc(i, block).start()
+
+    def weight_keep(i, left, right):
+        own_half = slots(i)[0]
+
+        def here(j, carry):
+            own_half[half_rows(j), :] = weight_part(left, right, y, j)
+            return carry
+
         lax.fori_loop(0, 3, here, 0)
 
     def z_rows(block):
@@ -941,7 +953,7 @@
             TBS[1, 0, i] = made[TAB : 2 * TAB].astype(BF)
             return carry
 
-        lax.fori_loop(0, 3, body, 0)
+        lax.fori_loop(0, 3, body, 0, unroll=True)
 
     def pair(ext, s):
         ext = ext.astype(F32)
@@ -966,7 +978,7 @@
             GVL[i] = tn(SS[i], ext)
             return carry
 
-        lax.fori_loop(0, 3, body, 0)
+        lax.fori_loop(0, 3, body, 0, unroll=True)
         RGQ[s] = side_by_side(GM3)
 
     def back_keys(s):
@@ -981,7 +993,7 @@
             GV3[h] = gv + jnp.where(CM[1, s] > 0, cross[:, 128:256], 0.0)
             return carry
 
-        lax.fori_loop(0, 3, body, 0)
+        lax.fori_loop(0, 3, body, 0, unroll=True)
         RGK[s] = side_by_side(GM3)
         RGV[s] = side_by_side(GV3)
 
@@ -991,120 +1003,133 @@
             P[s, :, tile(j)] = made + nt(RGV[s], WV[tile(j), :])
             return carry
 
-        lax.fori_loop(0, 3, body, 0)
-
+        lax.fori_loop(0, 3, body, 0, unroll=True)
+
+    w_send(4)
     w_send(3)
-    w_send(4)
+    w_send(5)
     w_pass(2)
+    w_over(3)
+    w_over(4)
+    w_over(5)
     w_wait(0)
     w_wait(1)
     ag_wait(0, X, 0)
     project_keys(0)
     keys(0)
     tb_send(0, 0)
-    w_relay(4, 0)
-    w_pass(3)
     ag_wait(0, X, 1)
     project_keys(1)
     keys(1)
     tb_send(0, 1)
-    w_relay(4, 1)
+    w_pass(3)
     w_wait(2)
     project_queries(0)
     queries(0)
-    w_relay(4, 2)
+    tb_relay(0, 0)
     project_queries(1)
     queries(1)
-    w_send(5)
+    tb_relay(0, 1)
+    w_relay(4, 0)
+    w_relay(5, 0)
     mixing(0)
     w_wait(3)
     attn_out(0)
     rs_start(0, 0)
     mixing(1)
     attn_out(1)
+    rs_mid(0, 0)
     rs_start(0, 1)
-    rs_mid(0, 0)
+    w_relay(4, 1)
     rs_mid(0, 1)
-    w_relay(5, 0)
     norm_one(0, rs_fin(0, 0))
     ag_start(1, FI, 0)
+    w_relay(5, 1)
     norm_one(1, rs_fin(0, 1))
     ag_start(1, FI, 1)
-    w_relay(5, 1)
+    w_relay(4, 2)
     ag_pass(1, FI, 0)
-    ag_pass(1, FI, 1)
+    ag_wait(1, FI, 0)
     w_relay(5, 2)
-    ag_wait(1, FI, 0)
     w_wait(4)
     ffn_up(0)
+    ag_pass(1, FI, 1)
+    ag_wait(1, FI, 1)
+    ffn_up(1)
     w_wait(5)
     ffn_down(0)
     rs_start(1, 0)
-    ag_wait(1, FI, 1)
-    ffn_up(1)
+    ffn_down(1)
     rs_mid(1, 0)
-    ffn_down(1)
     rs_start(1, 1)
+    rs_mid(1, 1)
     norm_two(0, rs_fin(1, 0))
     ag_start(2, G2, 0)
-    rs_mid(1, 1)
     norm_two(1, rs_fin(1, 1))
     ag_start(2, G2, 1)
     ag_pass(2, G2, 0)
-    ag_pass(2, G2, 1)
     ag_wait(2, G2, 0)
     ffn_back_hidden(0)
+    ag_pass(2, G2, 1)
     ffn_back_rows(0)
     rs_start(2, 0)
     ag_wait(2, G2, 1)
+    weight_send(5, G2, HID)
+    rs_mid(2, 0)
     ffn_back_hidden(1)
-    rs_mid(2, 0)
     ffn_back_rows(1)
     rs_start(2, 1)
-    weight_grad(5, G2, HID)
+    weight_send(4, FI, GUP)
     rs_mid(2, 1)
     norm_one_back(0, rs_fin(2, 0))
     ag_start(3, G1, 0)
+    weight_keep(5, G2, HID)
     norm_one_back(1, rs_fin(2, 1))
     ag_start(3, G1, 1)
     ar_desc(0).start()
-    weight_grad(4, FI, GUP)
+    g_relay(5, 2)
     ag_pass(3, G1, 0)
-    g_relay(5, 2)
+    weight_keep(4, FI, GUP)
+    ag_wait(3, G1, 0)
+    grad_tables(0)
+    tb_send(1, 0)
     ag_pass(3, G1, 1)
     ar_take(0)
     ar_desc(1).start()
-    ag_wait(3, G1, 0)
-    grad_tables(0)
-    tb_send(1, 0)
     ag_wait(3, G1, 1)
     grad_tables(1)
     tb_send(1, 1)
-    weight_grad(3, G1, MIXC)
+    weight_send(3, G1, MIXC)
     g_relay(5, 1)
+    back_queries(0)
+    tb_relay(1, 0)
     ar_take(1)
     ar_desc(2).start()
-    back_queries(0)
+    back_queries(1)
+    tb_relay(1, 1)
+    weight_send(2, X, RGQ)
     g_relay(5, 0)
-    back_queries(1)
-    weight_grad(2, X, RGQ)
-    g_relay(4, 2)
+    weight_keep(3, G1, MIXC)
+    weight_keep(2, X, RGQ)
     ar_take(2)
     ar_z_start()
+    g_relay(4, 2)
     back_keys(0)
-    g_relay(4, 1)
     input_rows(0)
     rs_start(3, 0)
+    g_relay(4, 1)
     back_keys(1)
     rs_mid(3, 0)
-    weight_grad(0, X, RGK)
-    weight_grad(1, X, RGV)
-    g_relay(4, 0)
+    weight_send(0, X, RGK)
+    weight_send(1, X, RGV)
     input_rows(1)
     rs_start(3, 1)
     g_pass(3)
+    weight_keep(0, X, RGK)
+    weight_keep(1, X, RGV)
+    g_relay(4, 0)
+    rs_mid(3, 1)
     g_pass(2)
-    rs_mid(3, 1)
     g_pass(0)
     g_pass(1)
     gin_ref[0] = (GH1[0] + rs_fin(3, 0)).astype(BF)
@@ -1126,7 +1151,16 @@
             sib_desc(op, s, 1).wait_send()
             xrs_desc(op, s).wait_send()
         for way in range(2):
-            tb_each(lambda side, dist: tb_desc(way, s, side, dist).wait_send())
+            for side in range(2):
+
+                @pl.when(reaches(1 - side, 1))
+                def _():
+                    tb_desc(way, s, side, 1).wait_send()
+
+                @pl.when((z == 1) | (z == 2))
+                def _():
+                    tb_desc(way, s, side, 2).wait_send()
+
     for i in range(6):
         wy_desc(i, 0).wait_send()
         for block in range(4):
@@ -1162,11 +1196,10 @@
     out_ref, gin_ref, ok_ref, ov_ref, oq_ref, oo_ref, ou_ref, od_ref, small_ref,
     out_o, gin_o, q_o, k_o, v_o, o_o, ga_o, sa_o, u_o, bu_o, d_o, bd_o, gf_o, sf_o,
 ):
-    pairs = ((out_o, out_ref), (gin_o, gin_ref), (q_o, oq_ref), (k_o, ok_ref), (v_o, ov_ref), (u_o, ou_ref))
-    for dst, src in pairs:
+    narrow = ((q_o, oq_ref), (k_o, ok_ref), (v_o, ov_ref))
+    for dst, src in narrow + ((out_o, out_ref), (gin_o, gin_ref), (u_o, ou_ref), (d_o, od_ref)):
         dst[...] = src[...]
     o_o[...] = oo_ref[...].T
-    d_o[...] = od_ref[...].T
     for row, dst in enumerate((ga_o, sa_o, gf_o, sf_o, bd_o, bu_o)):
         dst[...] = small_ref[row, :]
 
@@ -1183,7 +1216,7 @@
     scratch = [
         vm((2, 256, 768), BF), vm((2, 256, 768), BF), vm((2, 256, 768), BF), vm((2, 256, 768), BF),
         vm((768, 192), BF), vm((768, 192), BF), vm((768, 192), BF), vm((768, 192), BF),
-        vm((768, 768), BF), vm((768, 768), BF), vm((96, 192), BF), vm((96, 768), BF),
+        vm((768, 768), BF), vm((768, 768), BF), vm((96, 192), BF),
         vm((2, 256, 768), F32), vm((2, 256, 768), BF), vm((2, 256, 768), F32), vm((2, 256, 768), BF),
         vm((2, 64, 768), F32), vm((2, 64, 768), F32), vm((2, 64, 128), F32),
         vm((2, 64, 768), F32), vm((2, 64, 768), F32),
@@ -1223,17 +1256,18 @@
         ),
     )(
         inputs, seg_ids, feature_map, w_query, w_key, w_value, w_out, gain_attn, shift_attn,
-        w_up, bias_up, w_down, bias_down, gain_ffn, shift_ffn, cotangent,
-    )
-    return pl.pallas_call(
+        w_up, bias_up, w_down.T, bias_down, gain_ffn, shift_ffn, cotangent,
+    )
+    done = pl.pallas_call(
         hand_out,
         out_shape=(
             rows, rows, narrow, narrow, narrow, shape((192, 96), F32), vec, vec,
-            wide, vec, shape((768, 96), F32), vec, vec, vec,
+            wide, vec, wide, vec, vec, vec,
         ),
         in_specs=[in_vmem] * 9,
         out_specs=(in_vmem,) * 14,
     )(*made)
+    return (*done[:10], done[10].T, *done[11:])
 
 
 def solution(mesh):

time: 164 us -> 146 us (0.89)
  Pallas kernels: 160 us -> 145 us
  local copies, waits for them, and re-layouts: 3.59 us -> 0 us
    pallas_call x1, Pallas kernels: 157 us -> 143 us  [fast_device(): pl.pallas_call(layer_kernel, out_shape=(rows, rows, narrow, narrow, narro...]
    pallas_call x1 -> x0, local copies, waits for them, and re-layouts: 1.87 us -> none  [fast_device(): pl.pallas_call(hand_out, out_shape=(rows, rows, narrow, narrow, narrow, s...]
    unnamed x1 -> x0, local copies, waits for them, and re-layouts: 1.72 us -> none
where the time goes in v2:
time: 146 us
  Pallas kernels  145 us (99%)
    pallas_call x1, Pallas kernels, fast_device(): pl.pallas_call(layer_kernel, out_shape=(rows, rows, narrow, narrow, narro...  143 us

profile of v2, /device:TPU:0, one launch (start us, length us, event | category | flops | bytes accessed | tf_op | source)
XLA Modules:
  0.0 146.1 jit_solution(16267055110844931723)
XLA Ops:
  0.7 142.8 %shard_map.263 = (bf16[2,64,768]{2,1,0:T(8,128)(2,1)}, bf16[2,64,768]{2,1,0:T(8,128)(2,1)}, f32[96,192]{1,0:T(8,128)}, f32[96,192]{1,0:T(8,128)}, f32[96,192]{1,...) custom-call(bf16[2,64,768]{2,1,0:T(8,128)(2,1)} %x_ref.1, ...), custom_call_target="tpu_custom_call" | custom-call | tf_op jit(solution)/shard_map/pallas_call | solution.py:1248
  143.5 2.5 %shard_map.264 = (bf16[2,64,768]{2,1,0:T(8,128)(2,1)}, bf16[2,64,768]{2,1,0:T(8,128)(2,1)}, f32[96,192]{1,0:T(8,128)}, f32[96,192]{1,0:T(8,128)}, f32[96,192]{1,...) custom-call(bf16[2,64,768]{2,1,0:T(8,128)(2,1)} %get-tuple-element.3, ...), custom_call_target="tpu_custom_call" | custom-call | tf_op jit(solution)/shard_map/pallas_call | solution.py:1261

commit v3 on v2

--- a/solution.py
+++ b/solution.py
@@ -579,9 +579,9 @@
 
     lax.fori_loop(0, 3, split_omega, 0)
 
-    for s in range(2):
-        ag_pass(0, X, s)
     w_pass(0)
+    ag_pass(0, X, 0)
+    ag_pass(0, X, 1)
     w_pass(1)
 
     for d in (1, 2, 3):
@@ -1054,13 +1054,13 @@
     w_wait(4)
     ffn_up(0)
     ag_pass(1, FI, 1)
-    ag_wait(1, FI, 1)
-    ffn_up(1)
     w_wait(5)
     ffn_down(0)
     rs_start(1, 0)
+    ag_wait(1, FI, 1)
+    ffn_up(1)
+    rs_mid(1, 0)
     ffn_down(1)
-    rs_mid(1, 0)
     rs_start(1, 1)
     rs_mid(1, 1)
     norm_two(0, rs_fin(1, 0))
@@ -1099,37 +1099,37 @@
     ag_wait(3, G1, 1)
     grad_tables(1)
     tb_send(1, 1)
+    ar_take(1)
+    ar_desc(2).start()
     weight_send(3, G1, MIXC)
     g_relay(5, 1)
     back_queries(0)
     tb_relay(1, 0)
-    ar_take(1)
-    ar_desc(2).start()
     back_queries(1)
+    g_relay(4, 2)
     tb_relay(1, 1)
     weight_send(2, X, RGQ)
-    g_relay(5, 0)
     weight_keep(3, G1, MIXC)
     weight_keep(2, X, RGQ)
-    ar_take(2)
-    ar_z_start()
-    g_relay(4, 2)
+    g_relay(5, 0)
     back_keys(0)
     input_rows(0)
     rs_start(3, 0)
-    g_relay(4, 1)
     back_keys(1)
     rs_mid(3, 0)
     weight_send(0, X, RGK)
     weight_send(1, X, RGV)
+    g_relay(4, 1)
     input_rows(1)
     rs_start(3, 1)
-    g_pass(3)
     weight_keep(0, X, RGK)
     weight_keep(1, X, RGV)
-    g_relay(4, 0)
+    ar_take(2)
+    ar_z_start()
+    g_pass(3)
     rs_mid(3, 1)
     g_pass(2)
+    g_relay(4, 0)
     g_pass(0)
     g_pass(1)
     gin_ref[0] = (GH1[0] + rs_fin(3, 0)).astype(BF)

time: 146 us -> 136 us (0.932)
  Pallas kernels: 145 us -> 135 us
    pallas_call x1, Pallas kernels: 143 us -> 133 us  [fast_device(): pl.pallas_call(layer_kernel, out_shape=(rows, rows, narrow, narrow, narro...]
where the time goes in v3:
time: 136 us
  Pallas kernels  135 us (99%)
    pallas_call x1, Pallas kernels, fast_device(): pl.pallas_call(layer_kernel, out_shape=(rows, rows, narrow, narrow, narro...  133 us

profile of v3, /device:TPU:0, one launch (start us, length us, event | category | flops | bytes accessed | tf_op | source)
XLA Modules:
  0.0 135.9 jit_solution(6534814611362134261)
XLA Ops:
  0.7 132.6 %shard_map.263 = (bf16[2,64,768]{2,1,0:T(8,128)(2,1)}, bf16[2,64,768]{2,1,0:T(8,128)(2,1)}, f32[96,192]{1,0:T(8,128)}, f32[96,192]{1,0:T(8,128)}, f32[96,192]{1,...) custom-call(bf16[2,64,768]{2,1,0:T(8,128)(2,1)} %x_ref.1, ...), custom_call_target="tpu_custom_call" | custom-call | tf_op jit(solution)/shard_map/pallas_call | solution.py:1248
  133.3 2.5 %shard_map.264 = (bf16[2,64,768]{2,1,0:T(8,128)(2,1)}, bf16[2,64,768]{2,1,0:T(8,128)(2,1)}, f32[96,192]{1,0:T(8,128)}, f32[96,192]{1,0:T(8,128)}, f32[96,192]{1,...) custom-call(bf16[2,64,768]{2,1,0:T(8,128)(2,1)} %get-tuple-element.3, ...), custom_call_target="tpu_custom_call" | custom-call | tf_op jit(solution)/shard_map/pallas_call | solution.py:1261
